TPU v7x, 32 devices: a whole 2x2x4 slice. The times are simulated.
32 devices in a mesh: seq: 8 (over z, core), batch: 4 (over y, x).
Axes of the slice: x: 2, y: 2, z: 4, core: 2. Of those that a mesh axis runs over, the one named last changes fastest.
Arguments:
- inputs: bfloat16 [4, 64, 8192], P('batch'), may hold values from -6 to 6
- w_query: bfloat16 [8192, 8192], P('batch', 'seq'), may hold values from -0.0625 to 0.0625
- cache_keys: bfloat16 [4, 4096, 1024], P('batch', 'seq'), may hold values from -120 to 120
- cache_values: bfloat16 [4, 4096, 1024], P('batch', 'seq'), may hold values from -6 to 6
- lengths: int32 [4], P('batch'), may hold values from 1 to 4096, as said below
- positions: int32 [4, 64], P('batch'), may hold values from 0 to 4095, as said below
Outputs:
- attended: bfloat16 [4, 64, 8192], P('batch', None, 'seq')
Inputs may be any that keep to these rules, and one draw needn't show every extreme that they name: `lengths`: every sample has at least one valid position; some sample has all 4096 valid. `positions`: some query sits at position 0 and some at 4095.
All inputs are finite; a program needn't handle non-finite values.
Results may differ from a plain program's by a relative error of at most 0.015.
The roundings to bfloat16 on the way count: a program that leaves them out, or rounds other values in their place, can miss the bound.
Values may be sent and summed in bfloat16 or wider, within the bound.
No kernel may reach another device: no remote copies, remote signals or barrier semaphores. Data moves between devices by JAX's collectives and lax.ppermute only.
A program may use at most 64 MiB of HBM per device.

v0:
```python
import functools

import jax
import jax.numpy as jnp
from jax import lax
from jax.experimental import pallas as pl
from jax.experimental.pallas import tpu as pltpu
from jax.sharding import PartitionSpec as P


H = 64
KVH = 8
HD = 128


ANY = pl.BlockSpec(memory_space=pl.ANY)
HBM = pl.BlockSpec(memory_space=pltpu.HBM)
VMEM = pl.BlockSpec(memory_space=pltpu.VMEM)
SMEM = pl.BlockSpec(memory_space=pltpu.SMEM)
PARTNERS = 2
SMALL = pltpu.CompilerParams(vmem_limit_bytes=24 << 20)
LOG2E = 1.4426950408889634
NONE_VISIBLE = -1e30


def peers(count, step):
    if count & (count - 1) == 0:
        return [(j, j ^ step) for j in range(count)]
    return [(j, (j + step) % count) for j in range(count)]


def target(me, count, step):
    return me ^ step if count & (count - 1) == 0 else lax.rem(me + step, count)


def source(me, count, step):
    return me ^ step if count & (count - 1) == 0 else lax.rem(me + count - step, count)


def seq_order(count):
    half = count // 2
    far = [*range(half + 2, count, 2), *range(half + 1, count, 2)]
    return [half, *range(2, half), *far, 1]


def pack(key_rows, value_rows, tokens, seq_count, batch_count, steps):
    keys_here, width = key_rows.shape
    share = width // seq_count
    sources = [key_rows, value_rows] + ([] if tokens is None else [tokens])
    shapes = [jax.ShapeDtypeStruct((2, keys_here, share), key_rows.dtype)] * len(steps)
    if tokens is not None:
        depth = tokens.shape[1] // batch_count
        widths = [depth] + [depth // 2] * (batch_count - 1)
        shapes = shapes + [jax.ShapeDtypeStruct((tokens.shape[0], width), tokens.dtype) for width in widths]

    def kernel(*refs):
        ins, outs, sem = refs[: len(sources)], refs[len(sources) : -1], refs[-1]
        copies = []

        def move(ref, start, size, out):
            columns = pl.ds(pl.multiple_of(start, HD), size)
            copy = pltpu.make_async_copy(ref.at[:, columns], out, sem.at[len(copies)])
            copy.start()
            copies.append(copy)

        if tokens is not None:
            me, half = lax.axis_index("batch"), lax.rem(lax.axis_index("seq"), 2)
            for step, width in enumerate(widths):
                start = target(me, batch_count, step) * depth + (half * width if step else 0)
                move(ins[2], start, width, outs[len(steps) + step])
        me = lax.axis_index("seq")
        for n, step in enumerate(steps):
            for part in range(2):
                move(ins[part], target(me, seq_count, step) * share, share, outs[n].at[part])
        for copy in copies:
            copy.wait()

    n_copies = 2 * len(steps) + (0 if tokens is None else batch_count)
    out = pl.pallas_call(
        kernel,
        out_shape=shapes,
        in_specs=[HBM] * len(sources),
        out_specs=[VMEM] * len(shapes),
        scratch_shapes=[pltpu.SemaphoreType.DMA((n_copies,))],
        cost_estimate=pl.CostEstimate(
            flops=0, transcendentals=0, bytes_accessed=len(steps) * 8 * keys_here * share
        ),
        compiler_params=SMALL,
    )(*sources)
    return list(out)


def project(own, halves, other_halves, weight):
    count = 1 + len(halves)
    rows, depth = own.shape
    columns = weight.shape[1]
    tile = min(256, columns)

    def kernel(*refs):
        ins, w_ref, outs, stacked = refs[: 2 * count - 1], refs[2 * count - 1], refs[2 * count : -1], refs[-1]

        @pl.when(pl.program_id(0) == 0)
        def _():
            mine = lax.rem(lax.axis_index("seq"), 2)
            stacked[:rows, :] = ins[0][...]
            for n in range(1, count):
                for which, ref in ((mine, ins[n]), (1 - mine, ins[count - 1 + n])):
                    start = pl.multiple_of(which * (depth // 2), HD)
                    stacked[n * rows : (n + 1) * rows, pl.ds(start, depth // 2)] = ref[...]

        product = jnp.dot(stacked[...], w_ref[...], preferred_element_type=jnp.float32)
        for n in range(count):
            outs[n][...] = product[n * rows : (n + 1) * rows]

    return pl.pallas_call(
        kernel,
        grid=(columns // tile,),
        out_shape=[jax.ShapeDtypeStruct((rows, columns), jnp.float32)] * count,
        in_specs=[pl.BlockSpec((rows, depth), lambda j: (0, 0))]
        + [pl.BlockSpec((rows, depth // 2), lambda j: (0, 0))] * (2 * count - 2)
        + [pl.BlockSpec((depth, tile), lambda j: (0, j))],
        out_specs=[pl.BlockSpec((rows, tile), lambda j: (0, j))] * count,
        scratch_shapes=[pltpu.VMEM((count * rows, depth), own.dtype)],
        cost_estimate=pl.CostEstimate(
            flops=2 * count * rows * depth * columns,
            transcendentals=0,
            bytes_accessed=2 * depth * columns + 6 * count * rows * depth,
        ),
        compiler_params=SMALL,
        name="project",
    )(own, *halves, *other_halves, weight)


def swapped(me, pairs):
    other = me
    for one, two in pairs:
        other = jnp.where(me == one, two, jnp.where(me == two, one, other))
    return other


def round_query(partials):
    tokens, width = partials[0].shape
    group = width // HD

    def kernel(*refs):
        ins, out, held, sem = refs[: len(partials)], refs[len(partials)], refs[len(partials) + 1 : -1], refs[-1]
        copies = [pltpu.make_async_copy(src, dst, sem.at[n]) for n, (src, dst) in enumerate(zip(ins, held))]
        for copy in copies:
            copy.start()
        for copy in copies:
            copy.wait()
        for h in range(group):
            head = slice(h * HD, (h + 1) * HD)
            total = held[0][:, head]
            for ref in held[1:]:
                total = total + ref[:, head]
            out[h * tokens : (h + 1) * tokens, :] = total.astype(jnp.bfloat16)

    return pl.pallas_call(
        kernel,
        out_shape=jax.ShapeDtypeStruct((group * tokens, HD), jnp.bfloat16),
        in_specs=[ANY] * len(partials),
        out_specs=VMEM,
        scratch_shapes=[pltpu.VMEM(x.shape, x.dtype) for x in partials]
        + [pltpu.SemaphoreType.DMA((len(partials),))],
        cost_estimate=pl.CostEstimate(
            flops=len(partials) * tokens * width,
            transcendentals=0,
            bytes_accessed=4 * len(partials) * tokens * width,
        ),
        compiler_params=SMALL,
        name="round_query",
    )(*partials)


def merge(top, denom, numer, other_top, other_denom, other_numer):
    new_top = jnp.maximum(top, other_top)
    keep = jnp.exp2((top - new_top) * (HD**-0.5 * LOG2E))
    weight = jnp.exp2((other_top - new_top) * (HD**-0.5 * LOG2E))
    return new_top, denom * keep + other_denom * weight, numer * keep + other_numer * weight


def read_state(ref, part=slice(None)):
    if ref.dtype == jnp.bfloat16:
        parts = ref[HD:, part].astype(jnp.float32)
        top, denom = (parts[n : n + 1] + parts[n + 1 : n + 2] + parts[n + 2 : n + 3] for n in (0, 3))
        return top, denom, ref[:HD, part].astype(jnp.float32)
    return ref[HD : HD + 1, part], ref[HD + 8 : HD + 9, part], ref[:HD, part]


def exact_parts(x):
    high = x.astype(jnp.bfloat16).astype(jnp.float32)
    middle = (x - high).astype(jnp.bfloat16).astype(jnp.float32)
    return high, middle, x - high - middle


def attend(queries, chunks, steps, state, positions, lengths, seq_count, pairs, send=False):
    first = state is None
    tokens = positions.shape[1]
    columns = queries[0].shape[0]
    n_query = len(queries)
    n_chunks = len(chunks)
    keys_here = chunks[0].shape[-2]
    moved = [*queries, *chunks]
    inputs = [lengths, positions, *moved] + ([] if first else [state])

    def kernel(*refs):
        lengths_ref, positions_ref = refs[:2]
        moved_refs = refs[2 : 2 + len(moved)]
        out = refs[len(inputs)]
        held = refs[len(inputs) + 1 + send : -1]
        sem = refs[-1]
        copies = [
            pltpu.make_async_copy(src, dst, sem.at[n]) for n, (src, dst) in enumerate(zip(moved_refs, held))
        ]
        for copy in copies:
            copy.start()
        me = lax.axis_index("seq")
        other = swapped(me, pairs)
        limit = jnp.minimum(positions_ref[...], lengths_ref[0] - 1)
        limit = jnp.concatenate([limit] * (columns // tokens), axis=1)
        rows = lax.broadcasted_iota(jnp.int32, (keys_here, columns), 0)
        for copy in copies[:n_query]:
            copy.wait()
        q = held[0][...]
        if n_query == 2:
            q = jnp.where(other == me, q, held[1][...])
        for copy in copies[n_query:]:
            copy.wait()
        wide, deep = min(columns, 256), min(keys_here, 128)
        for c in range(0, columns, wide):
            part = slice(c, c + wide)
            sums = None if first else read_state(refs[len(inputs) - 1], part)
            for n, step in enumerate(steps):
                start = source(other, seq_count, step) * keys_here
                ref = held[n_query + n]
                scores = []
                for r in range(0, keys_here, deep):
                    score = lax.dot_general(
                        ref[0, r : r + deep],
                        q[part],
                        (((1,), (1,)), ((), ())),
                        preferred_element_type=jnp.float32,
                    )
                    scores.append(jnp.where(rows[:deep, part] <= limit[:, part] - (start + r), score, NONE_VISIBLE))
                block_max = functools.reduce(
                    jnp.maximum, [jnp.max(score, axis=0, keepdims=True) for score in scores]
                )
                block_total, block_sum = 0.0, 0.0
                for r, score in zip(range(0, keys_here, deep), scores):
                    expo = jnp.exp2((score - block_max) * (HD**-0.5 * LOG2E))
                    block_total = block_total + jnp.sum(expo, axis=0, keepdims=True)
                    block_sum = block_sum + lax.dot_general(
                        ref[1, r : r + deep],
                        expo.astype(jnp.bfloat16),
                        (((0,), (0,)), ((), ())),
                        preferred_element_type=jnp.float32,
                    )
                block_sum = block_sum.astype(jnp.bfloat16).astype(jnp.float32)
                block = block_max, block_total, block_sum
                sums = block if sums is None else merge(*sums, *block)
            top, denom, numer = sums
            out[:HD, part] = numer
            out[HD : HD + 8, part] = jnp.broadcast_to(top, (8, wide))
            out[HD + 8 :, part] = jnp.broadcast_to(denom, (8, wide))
            if send:
                sent = refs[len(inputs) + 1]
                sent[:HD, part] = numer.astype(jnp.bfloat16)
                parts = jnp.concatenate([*exact_parts(top), *exact_parts(denom), jnp.zeros((10, wide))], axis=0)
                sent[HD:, part] = parts.astype(jnp.bfloat16)

    return pl.pallas_call(
        kernel,
        out_shape=[
            jax.ShapeDtypeStruct((HD + 16, columns), dtype) for dtype in (jnp.float32, jnp.bfloat16)[: 1 + send]
        ],
        in_specs=[SMEM, VMEM] + [ANY] * len(moved) + [VMEM] * (len(inputs) - 2 - len(moved)),
        out_specs=[VMEM] * (1 + send),
        scratch_shapes=[pltpu.VMEM(x.shape, x.dtype) for x in moved]
        + [pltpu.SemaphoreType.DMA((len(moved),))],
        cost_estimate=pl.CostEstimate(
            flops=4 * n_chunks * keys_here * columns * HD,
            transcendentals=n_chunks * keys_here * columns,
            bytes_accessed=n_chunks * 4 * keys_here * HD,
        ),
        compiler_params=SMALL,
        name="attend",
    )(*inputs)


def finish(near, far, received, tokens, pairs):
    columns = near.shape[1]
    group = columns // tokens

    def kernel(near_ref, far_ref, received_ref, out):
        me = lax.axis_index("seq")
        mine = swapped(me, pairs) == me
        far_sums = [
            jnp.where(mine, one, two) for one, two in zip(read_state(far_ref), read_state(received_ref))
        ]
        _, denom, numer = merge(*read_state(near_ref), *far_sums)
        result = numer / denom
        for h in range(group):
            part = result[:, h * tokens : (h + 1) * tokens]
            out[:, h * HD : (h + 1) * HD] = jnp.transpose(part).astype(jnp.bfloat16)

    return pl.pallas_call(
        kernel,
        out_shape=jax.ShapeDtypeStruct((tokens, group * HD), jnp.bfloat16),
        in_specs=[VMEM] * 3,
        out_specs=VMEM,
        cost_estimate=pl.CostEstimate(
            flops=8 * HD * columns, transcendentals=0, bytes_accessed=12 * HD * columns
        ),
        compiler_params=SMALL,
        name="finish",
    )(near, far, received)


def partner_pairs(count):
    half = count // 2
    across = half + half // 2
    return [(one, one ^ across) for one in range(half // 2, half)][:PARTNERS]


def own_heads(inputs, w_query, cache_keys, cache_values, lengths, positions):
    seq_count = lax.axis_size("seq")
    batch_count = lax.axis_size("batch")
    half = seq_count // 2
    order = seq_order(seq_count)
    pairs = partner_pairs(seq_count)
    swap = dict([*pairs, *((two, one) for one, two in pairs)])
    meet = [(one, swap.get(one, one ^ 1)) for one in range(seq_count)]
    key_rows, value_rows, tokens = (
        pltpu.with_memory_space_constraint(x[0], pltpu.HBM) for x in (cache_keys, cache_values, inputs)
    )
    packed = pack(key_rows, value_rows, tokens, seq_count, batch_count, order[:1])
    packed, blocks = packed[:1], packed[1:]
    packed += pack(key_rows, value_rows, None, seq_count, batch_count, [*order[1:], 0])
    moved = {0: packed[-1]}
    for step, block in zip(order, packed):
        to = peers(seq_count, step)
        if step >= half:
            to = [(a, swap.get(b, b)) for a, b in to]
        moved[step] = lax.ppermute(block, "seq", to)
    halves, other_halves = [], []
    for step in range(1, batch_count):
        halves.append(lax.ppermute(blocks[step], "batch", peers(batch_count, step)))
        other_halves.append(lax.ppermute(halves[-1], "seq", peers(seq_count, 1)))
    partials = project(blocks[0], halves, other_halves, w_query)
    back = [partials[0]]
    for step in range(1, batch_count):
        back.append(lax.ppermute(partials[step], "batch", [(b, a) for a, b in peers(batch_count, step)]))
    query = round_query(back)
    queries = [query]
    if pairs:
        queries.append(lax.ppermute(query, "seq", meet))
    attend_ = functools.partial(attend, positions=positions, lengths=lengths, seq_count=seq_count)
    early, far_steps = [*range(half)], [s for s in order if s >= half]
    near = None
    for steps in (early[:-1], early[-1:]):
        (near,) = attend_([query], [moved[s] for s in steps], steps, near, pairs=[])
    far = attend_(queries, [moved[s] for s in far_steps], far_steps, None, pairs=pairs, send=bool(pairs))
    received = far[0]
    if pairs:
        received = lax.ppermute(far[1], "seq", meet)
    return finish(near, far[0], received, positions.shape[1], pairs)[None]


def split_positions(inputs, w_query, cache_keys, cache_values, lengths, positions):
    seq_count = lax.axis_size("seq")
    heads_here = H // seq_count
    group = H // KVH
    keys_here = cache_keys.shape[1]
    tokens = inputs[0]
    query_rows = tokens.shape[0]
    features = lax.all_to_all(inputs, "batch", split_axis=2, concat_axis=0, tiled=True)
    query = lax.psum_scatter(
        jnp.einsum("sqd,dc->sqc", features, w_query, preferred_element_type=jnp.float32),
        "batch",
        scatter_dimension=0,
        tiled=True,
    )[0]
    query = query.astype(jnp.bfloat16)
    all_query = lax.all_gather(query, "seq", axis=1, tiled=True)
    query_heads = all_query.reshape(query_rows, KVH, group, HD)
    key_pos = lax.axis_index("seq") * keys_here + jnp.arange(keys_here, dtype=jnp.int32)
    visible = (key_pos[None, :] <= positions[0][:, None]) & (key_pos[None, :] < lengths[0])
    key_rows = cache_keys[0]
    value_rows = cache_values[0]

    def one_head(kv_head):
        key_block = lax.dynamic_slice_in_dim(key_rows, kv_head * HD, HD, 1)
        value_block = lax.dynamic_slice_in_dim(value_rows, kv_head * HD, HD, 1)
        query_group = lax.dynamic_index_in_dim(query_heads, kv_head, 1, keepdims=False)
        score = jnp.einsum(
            "qrd,kd->rqk", query_group, key_block, preferred_element_type=jnp.float32
        ) * HD ** (-0.5)
        block_max = jnp.max(jnp.where(visible[None], score, -1e30), axis=-1)
        expo = jnp.where(visible[None], jnp.exp(score - block_max[..., None]), 0.0)
        block_total = jnp.sum(expo, axis=-1)
        prob = expo.astype(jnp.bfloat16)
        block_sum = jnp.einsum(
            "rqk,kd->rqd", prob, value_block, preferred_element_type=jnp.float32
        ).astype(jnp.bfloat16)
        return (block_sum, block_max, block_total)

    sums, maxima, totals = lax.map(one_head, jnp.arange(KVH, dtype=jnp.int32))
    sums = sums.reshape(1, H, query_rows, HD)
    maxima = maxima.reshape(1, H, query_rows)
    totals = totals.reshape(1, H, query_rows)
    got_sums = lax.all_to_all(sums, "seq", split_axis=1, concat_axis=0, tiled=True)
    got_max, got_total = (
        lax.all_to_all(maxima, "seq", split_axis=1, concat_axis=0, tiled=True),
        lax.all_to_all(totals, "seq", split_axis=1, concat_axis=0, tiled=True),
    )
    top = jnp.max(got_max, axis=0)
    weight = jnp.exp(got_max - top[None])
    numer = jnp.sum(weight[..., None] * got_sums.astype(jnp.float32), axis=0)
    denom = jnp.sum(weight * got_total, axis=0)
    result = numer / denom[..., None]
    return (
        jnp.transpose(result, (1, 0, 2))
        .reshape(query_rows, heads_here * HD)[None]
        .astype(jnp.bfloat16)
    )


def solution(mesh):
    in_specs = (
        P("batch", None, None),
        P("batch", "seq"),
        P("batch", "seq", None),
        P("batch", "seq", None),
        P("batch"),
        P("batch", None),
    )
    out_specs = P("batch", None, "seq")
    split = functools.partial(
        jax.shard_map, mesh=mesh, in_specs=in_specs, out_specs=out_specs, check_vma=False
    )
    if mesh.shape["seq"] != KVH:
        return split(split_positions)
    return split(own_heads)
```

profile of v0, /device:TPU:0, one launch (start us, length us, event | category | flops | bytes accessed | tf_op | source)
XLA Modules:
  0.0 61.6 jit_solution(16259218466663084138)
XLA Ops:
  0.0 1.2 %shard_map.64 = (bf16[2,512,128]{2,1,0:T(8,128)(2,1)S(1)}, bf16[64,2048]{1,0:T(8,128)(2,1)S(1)}, bf16[64,1024]{1,0:T(8,128)(2,1)S(1)}, bf16[64,1024]{1,0:T(8,128)(2,1)S(1)}, bf16[64,1024]{1,0:T(8,128)(2,1)S(1)}) custom-call(bf16[512,1024]{1,0:T(8,128)(2,1)} %bitcast.4, bf16[512,1024]{1,0:T(8,128)(2,1)} %bitcast.6, bf16[64,8192]{1,0:T(8,128)(2,1)} %bitcast.8), custom_call_target="tpu_custom_call" | custom-call | bytes 524288 | tf_op jit(solution)/shard_map/pallas_call | solution.py:79
  1.3 3.0 %collective-permute-start = (bf16[64,1024]{1,0:T(8,128)(2,1)S(1)}, bf16[64,1024]{1,0:T(8,128)(2,1)S(1)}, u32[]{:S(2)}, u32[]{:S(2)}) collective-permute-start(bf16[64,1024]{1,0:T(8,128)(2,1)S(1)} %get-tuple-element.24), channel_id=1, source_target_pairs={{0,1},{1,0},{2,3},{3,2},{4,5},{5,4},{6,7},{7,6},{8,9},{9,8},{10,11... | collective-permute-start | bytes 393224 | tf_op jit(solution)/shard_map/ppermute | solution.py:348
  4.3 1.5 %collective-permute-start.1 = (bf16[64,1024]{1,0:T(8,128)(2,1)S(1)}, bf16[64,1024]{1,0:T(8,128)(2,1)S(1)}, u32[]{:S(2)}, u32[]{:S(2)}) collective-permute-start(bf16[64,1024]{1,0:T(8,128)(2,1)S(1)} %get-tuple-element.25), channel_id=1, source_target_pairs={{0,2},{1,3},{2,0},{3,1},{4,6},{5,7},{6,4},{7,5},{8,10},{9,11},{10,... | collective-permute-start | bytes 393224 | tf_op jit(solution)/shard_map/ppermute | solution.py:348
  5.8 2.3 %collective-permute-done.refs_1_ = bf16[64,1024]{1,0:T(8,128)(2,1)S(1)} collective-permute-done((bf16[64,1024]{1,0:T(8,128)(2,1)S(1)}, bf16[64,1024]{1,0:T(8,128)(2,1)S(1)}, u32[]{:S(2)}, u32[]{:S(2)}) %collective-permute-start) | collective-permute-done | bytes 131104 | tf_op jit(solution)/shard_map/ppermute | solution.py:348
  8.2 3.9 %collective-permute-done.1.refs_2_ = bf16[64,1024]{1,0:T(8,128)(2,1)S(1)} collective-permute-done((bf16[64,1024]{1,0:T(8,128)(2,1)S(1)}, bf16[64,1024]{1,0:T(8,128)(2,1)S(1)}, u32[]{:S(2)}, u32[]{:S(2)}) %collective-permute-start.1) | collective-permute-done | bytes 131104 | tf_op jit(solution)/shard_map/ppermute | solution.py:348
  12.1 0.5 collective-permute-start.5
  12.6 0.8 %collective-permute-done.4.refs_5_ = bf16[64,1024]{1,0:T(8,128)(2,1)S(1)} collective-permute-done((bf16[64,1024]{1,0:T(8,128)(2,1)S(1)}, bf16[64,1024]{1,0:T(8,128)(2,1)S(1)}, u32[]{:S(2)}, u32[]{:S(2)}) %collective-permute-start.4) | collective-permute-done | bytes 131104 | tf_op jit(solution)/shard_map/ppermute | solution.py:349
  13.4 0.2 collective-permute-done.5.refs_6_
  13.6 2.2 %copy-done = bf16[2048,1024]{1,0:T(8,128)(2,1)S(1)} copy-done((bf16[2048,1024]{1,0:T(8,128)(2,1)S(1)}, bf16[2048,1024]{1,0:T(8,128)(2,1)}, u32[]{:S(2)}) %copy-start) | copy-done | bytes 4194328
  15.8 2.6 %project.1 = (f32[64,1024]{1,0:T(8,128)S(1)}, f32[64,1024]{1,0:T(8,128)S(1)}, f32[64,1024]{1,0:T(8,128)S(1)}, f32[64,1024]{1,0:T(8,128)S(1)}) custom-call(bf16[64,2048]{1,0:T(8,128)(2,1)S(1)} %get-tuple-element.23.refs_0_, bf16[64,1024]{1,0:T(8,128)(2,1)S(1)} %collective-permute-done.refs_1_, bf16[64,1024]{1,0:T(8,128)(2,1)S(1)} %collective-permute-done.1.refs_2_, ...), custom_call_target="tpu_custom_call" | custom-call | flops 1073741824 | bytes 7340032 | tf_op jit(solution)/shard_map/project/pallas_call | solution.py:115
  18.4 1.1 %collective-permute-start.6 = (f32[64,1024]{1,0:T(8,128)S(1)}, f32[64,1024]{1,0:T(8,128)S(1)}, u32[]{:S(2)}, u32[]{:S(2)}) collective-permute-start(f32[64,1024]{1,0:T(8,128)S(1)} %get-tuple-element.28), channel_id=1, source_target_pairs={{1,0},{0,1},{3,2},{2,3},{5,4},{4,5},{7,6},{6,7},{9,8},{8,9},{11,10... | collective-permute-start | bytes 786440 | tf_op jit(solution)/shard_map/ppermute | solution.py:353
  19.5 1.0 %collective-permute-start.7 = (f32[64,1024]{1,0:T(8,128)S(1)}, f32[64,1024]{1,0:T(8,128)S(1)}, u32[]{:S(2)}, u32[]{:S(2)}) collective-permute-start(f32[64,1024]{1,0:T(8,128)S(1)} %get-tuple-element.29), channel_id=1, source_target_pairs={{2,0},{3,1},{0,2},{1,3},{6,4},{7,5},{4,6},{5,7},{10,8},{11,9},{8,1... | collective-permute-start | bytes 786440 | tf_op jit(solution)/shard_map/ppermute | solution.py:353
  20.5 1.4 %collective-permute-start.8 = (f32[64,1024]{1,0:T(8,128)S(1)}, f32[64,1024]{1,0:T(8,128)S(1)}, u32[]{:S(2)}, u32[]{:S(2)}) collective-permute-start(f32[64,1024]{1,0:T(8,128)S(1)} %get-tuple-element.30), channel_id=1, source_target_pairs={{3,0},{2,1},{1,2},{0,3},{7,4},{6,5},{5,6},{4,7},{11,8},{10,9},{9,1... | collective-permute-start | bytes 786440 | tf_op jit(solution)/shard_map/ppermute | solution.py:353
  22.0 1.6 %collective-permute-start.13 = (bf16[2,512,128]{2,1,0:T(8,128)(2,1)S(1)}, bf16[2,512,128]{2,1,0:T(8,128)(2,1)S(1)}, u32[]{:S(2)}, u32[]{:S(2)}) collective-permute-start(bf16[2,512,128]{2,1,0:T(8,128)(2,1)S(1)} %get-tuple-element.35), channel_id=1, source_target_pairs={{0,8},{4,12},{8,24},{12,28},{16,0},{20,4},{24,16},{28,20},{1,9},{5... | collective-permute-start | bytes 786440 | tf_op jit(solution)/shard_map/ppermute | solution.py:345
  23.5 1.7 %shard_map.65 = (bf16[2,512,128]{2,1,0:T(8,128)(2,1)S(1)}, bf16[2,512,128]{2,1,0:T(8,128)(2,1)S(1)}, bf16[2,512,128]{2,1,0:T(8,128)(2,1)S(1)}, bf16[2,512,128]{2...) custom-call(bf16[512,1024]{1,0:T(8,128)(2,1)} %bitcast.5, ...), custom_call_target="tpu_custom_call" | custom-call | bytes 3670016 | tf_op jit(solution)/shard_map/pallas_call | solution.py:79
  25.2 4.4 %collective-permute-start.14 = (bf16[2,512,128]{2,1,0:T(8,128)(2,1)S(1)}, bf16[2,512,128]{2,1,0:T(8,128)(2,1)S(1)}, u32[]{:S(2)}, u32[]{:S(2)}) collective-permute-start(bf16[2,512,128]{2,1,0:T(8,128)(2,1)S(1)} %get-tuple-element.36), channel_id=1, source_target_pairs={{0,24},{4,28},{8,8},{12,12},{16,16},{20,20},{24,0},{28,4},{1,25},{... | collective-permute-start | bytes 786440 | tf_op jit(solution)/shard_map/ppermute | solution.py:345
  29.7 2.2 %collective-permute-done.7.refs_2_ = f32[64,1024]{1,0:T(8,128)S(1)} collective-permute-done((f32[64,1024]{1,0:T(8,128)S(1)}, f32[64,1024]{1,0:T(8,128)S(1)}, u32[]{:S(2)}, u32[]{:S(2)}) %collective-permute-start.7) | collective-permute-done | bytes 262176 | tf_op jit(solution)/shard_map/ppermute | solution.py:353
  31.9 1.6 %collective-permute-done.8.refs_3_ = f32[64,1024]{1,0:T(8,128)S(1)} collective-permute-done((f32[64,1024]{1,0:T(8,128)S(1)}, f32[64,1024]{1,0:T(8,128)S(1)}, u32[]{:S(2)}, u32[]{:S(2)}) %collective-permute-start.8) | collective-permute-done | bytes 262176 | tf_op jit(solution)/shard_map/ppermute | solution.py:353
  33.6 0.2 round_query.1.refs_2_
  33.7 2.2 %collective-permute-start.12 = (bf16[512,128]{1,0:T(8,128)(2,1)S(1)}, bf16[512,128]{1,0:T(8,128)(2,1)S(1)}, u32[]{:S(2)}, u32[]{:S(2)}) collective-permute-start(bf16[512,128]{1,0:T(8,128)(2,1)S(1)} %round_query.1.refs_2_), channel_id=1, source_target_pairs={{0,4},{4,0},{8,16},{12,20},{16,8},{20,12},{24,28},{28,24},{1,5},{5... | collective-permute-start | bytes 393224 | tf_op jit(solution)/shard_map/ppermute | solution.py:357
  35.9 0.1 collective-permute-start.10
  36.0 2.3 %collective-permute-done.14.refs_5_ = bf16[2,512,128]{2,1,0:T(8,128)(2,1)S(1)} collective-permute-done((bf16[2,512,128]{2,1,0:T(8,128)(2,1)S(1)}, bf16[2,512,128]{2,1,0:T(8,128)(2,1)S(1)}, u32[]{:S(2)}, u32[]{:S(2)}) %collective-permute-start.14) | collective-permute-done | bytes 262176 | tf_op jit(solution)/shard_map/ppermute | solution.py:345
  38.3 5.7 %collective-permute-done.15.refs_6_ = bf16[2,512,128]{2,1,0:T(8,128)(2,1)S(1)} collective-permute-done((bf16[2,512,128]{2,1,0:T(8,128)(2,1)S(1)}, bf16[2,512,128]{2,1,0:T(8,128)(2,1)S(1)}, u32[]{:S(2)}, u32[]{:S(2)}) %collective-permute-start.15) | collective-permute-done | bytes 262176 | tf_op jit(solution)/shard_map/ppermute | solution.py:345
  44.0 0.1 collective-permute-start.9
  44.8 2.9 %collective-permute-done.16.refs_7_ = bf16[2,512,128]{2,1,0:T(8,128)(2,1)S(1)} collective-permute-done((bf16[2,512,128]{2,1,0:T(8,128)(2,1)S(1)}, bf16[2,512,128]{2,1,0:T(8,128)(2,1)S(1)}, u32[]{:S(2)}, u32[]{:S(2)}) %collective-permute-start.16) | collective-permute-done | bytes 262176 | tf_op jit(solution)/shard_map/ppermute | solution.py:345
  47.7 2.6 %attend.5 = (f32[144,512]{1,0:T(8,128)S(1)}, bf16[144,512]{1,0:T(8,128)(2,1)S(1)}) custom-call(s32[1]{0:T(128)S(6)} %copy.7.refs_0_, s32[1,64]{1,0:T(1,128)S(1)} %copy-done.1, bf16[512,128]{1,0:T(8,128)(2,1)S(1)} %round_query.1.refs_2_, bf16[512,128]{1,0:T(8,128)(2,1)S(1)} %collective-permute-done.12.refs_3_, ...), custom_call_target="tpu_custom_call" | custom-call | flops 536870912 | bytes 1048576 | tf_op jit(solution)/shard_map/attend/pallas_call | solution.py:272
  50.3 1.8 %collective-permute-start.17 = (bf16[144,512]{1,0:T(8,128)(2,1)S(1)}, bf16[144,512]{1,0:T(8,128)(2,1)S(1)}, u32[]{:S(2)}, u32[]{:S(2)}) collective-permute-start(bf16[144,512]{1,0:T(8,128)(2,1)S(1)} %get-tuple-element.40), channel_id=1, source_target_pairs={{0,4},{4,0},{8,16},{12,20},{16,8},{20,12},{24,28},{28,24},{1,5},{5... | collective-permute-start | bytes 442376 | tf_op jit(solution)/shard_map/ppermute | solution.py:366
  52.2 2.1 %collective-permute-done.11.refs_5_ = bf16[2,512,128]{2,1,0:T(8,128)(2,1)S(1)} collective-permute-done((bf16[2,512,128]{2,1,0:T(8,128)(2,1)S(1)}, bf16[2,512,128]{2,1,0:T(8,128)(2,1)S(1)}, u32[]{:S(2)}, u32[]{:S(2)}) %collective-permute-start.11) | collective-permute-done | bytes 262176 | tf_op jit(solution)/shard_map/ppermute | solution.py:345
  54.2 1.9 %attend.3.refs_4_ = f32[144,512]{1,0:T(8,128)S(1)} custom-call(s32[1]{0:T(128)S(6)} %copy.7.refs_0_, s32[1,64]{1,0:T(1,128)S(1)} %copy-done.1, bf16[512,128]{1,0:T(8,128)(2,1)S(1)} %round_query.1.refs_2_, bf16[2,512,128]{2,1,0:T(8,128)(2,1)S(1)} %get-tuple-element.32.refs_3_, bf16[2,512,128]{2,1,0:T(8,128)(2,1)S(1)} %collective-permute-done.10.refs_4_, ...), custom_call_target="tpu_custom_call" | custom-call | flops 402653184 | bytes 786432 | tf_op jit(solution)/shard_map/attend/pallas_call | solution.py:272
  56.2 3.5 %collective-permute-done.9.refs_3_ = bf16[2,512,128]{2,1,0:T(8,128)(2,1)S(1)} collective-permute-done((bf16[2,512,128]{2,1,0:T(8,128)(2,1)S(1)}, bf16[2,512,128]{2,1,0:T(8,128)(2,1)S(1)}, u32[]{:S(2)}, u32[]{:S(2)}) %collective-permute-start.9) | collective-permute-done | bytes 262176 | tf_op jit(solution)/shard_map/ppermute | solution.py:345
  59.7 1.1 %attend.4.near_ref = f32[144,512]{1,0:T(8,128)S(1)} custom-call(s32[1]{0:T(128)S(6)} %copy.7.refs_0_, s32[1,64]{1,0:T(1,128)S(1)} %copy-done.1, bf16[512,128]{1,0:T(8,128)(2,1)S(1)} %round_query.1.refs_2_, bf16[2,512,128]{2,1,0:T(8,128)(2,1)S(1)} %collective-permute-done.9.refs_3_, f32[144,512]{1,0:T(8,128)S(1)} %attend.3.refs_4_), custom_call_target="tpu_custom_call" | custom-call | flops 134217728 | bytes 262144 | tf_op jit(solution)/shard_map/attend/pallas_call | solution.py:272
  60.7 0.9 %finish.1 = bf16[64,1024]{1,0:T(8,128)(2,1)} custom-call(f32[144,512]{1,0:T(8,128)S(1)} %attend.4.near_ref, f32[144,512]{1,0:T(8,128)S(1)} %get-tuple-element.39.far_ref, bf16[144,512]{1,0:T(8,128)(2,1)S(1)} %collective-permute-done.17.received_ref), custom_call_target="tpu_custom_call" | custom-call | flops 524288 | bytes 786432 | tf_op jit(solution)/shard_map/finish/pallas_call | solution.py:307
  (16 shorter events, 0.1 us)
Async XLA Ops:
  1.3 6.9 %collective-permute-start = (bf16[64,1024]{1,0:T(8,128)(2,1)S(1)}, bf16[64,1024]{1,0:T(8,128)(2,1)S(1)}, u32[]{:S(2)}, u32[]{:S(2)}) collective-permute-start(bf16[64,1024]{1,0:T(8,128)(2,1)S(1)} %get-tuple-element.24), channel_id=1, source_target_pairs={{0,1},{1,0},{2,3},{3,2},{4,5},{5,4},{6,7},{7,6},{8,9},{9,8},{10,11... | collective-permute-start | bytes 393224 | tf_op jit(solution)/shard_map/ppermute | solution.py:348
  4.3 7.8 %collective-permute-start.1 = (bf16[64,1024]{1,0:T(8,128)(2,1)S(1)}, bf16[64,1024]{1,0:T(8,128)(2,1)S(1)}, u32[]{:S(2)}, u32[]{:S(2)}) collective-permute-start(bf16[64,1024]{1,0:T(8,128)(2,1)S(1)} %get-tuple-element.25), channel_id=1, source_target_pairs={{0,2},{1,3},{2,0},{3,1},{4,6},{5,7},{6,4},{7,5},{8,10},{9,11},{10,... | collective-permute-start | bytes 393224 | tf_op jit(solution)/shard_map/ppermute | solution.py:348
  5.8 6.3 %collective-permute-start.2 = (bf16[64,1024]{1,0:T(8,128)(2,1)S(1)}, bf16[64,1024]{1,0:T(8,128)(2,1)S(1)}, u32[]{:S(2)}, u32[]{:S(2)}) collective-permute-start(bf16[64,1024]{1,0:T(8,128)(2,1)S(1)} %get-tuple-element.26), channel_id=1, source_target_pairs={{0,3},{1,2},{2,1},{3,0},{4,7},{5,6},{6,5},{7,4},{8,11},{9,10},{10,... | collective-permute-start | bytes 393224 | tf_op jit(solution)/shard_map/ppermute | solution.py:348
  8.2 4.4 %collective-permute-start.3 = (bf16[64,1024]{1,0:T(8,128)(2,1)S(1)}, bf16[64,1024]{1,0:T(8,128)(2,1)S(1)}, u32[]{:S(2)}, u32[]{:S(2)}) collective-permute-start(bf16[64,1024]{1,0:T(8,128)(2,1)S(1)} %collective-permute-done.refs_1_), channel_id=1, source_target_pairs={{0,4},{4,0},{8,12},{12,8},{16,20},{20,16},{24,28},{28,24},{1,5},{5... | collective-permute-start | bytes 393224 | tf_op jit(solution)/shard_map/ppermute | solution.py:349
  12.1 1.3 %collective-permute-start.4 = (bf16[64,1024]{1,0:T(8,128)(2,1)S(1)}, bf16[64,1024]{1,0:T(8,128)(2,1)S(1)}, u32[]{:S(2)}, u32[]{:S(2)}) collective-permute-start(bf16[64,1024]{1,0:T(8,128)(2,1)S(1)} %collective-permute-done.1.refs_2_), channel_id=1, source_target_pairs={{0,4},{4,0},{8,12},{12,8},{16,20},{20,16},{24,28},{28,24},{1,5},{5... | collective-permute-start | bytes 393224 | tf_op jit(solution)/shard_map/ppermute | solution.py:349
  12.1 1.5 %collective-permute-start.5 = (bf16[64,1024]{1,0:T(8,128)(2,1)S(1)}, bf16[64,1024]{1,0:T(8,128)(2,1)S(1)}, u32[]{:S(2)}, u32[]{:S(2)}) collective-permute-start(bf16[64,1024]{1,0:T(8,128)(2,1)S(1)} %collective-permute-done.2.refs_3_), channel_id=1, source_target_pairs={{0,4},{4,0},{8,12},{12,8},{16,20},{20,16},{24,28},{28,24},{1,5},{5... | collective-permute-start | bytes 393224 | tf_op jit(solution)/shard_map/ppermute | solution.py:349
  13.6 2.2 %copy-start = (bf16[2048,1024]{1,0:T(8,128)(2,1)S(1)}, bf16[2048,1024]{1,0:T(8,128)(2,1)}, u32[]{:S(2)}) copy-start(bf16[2048,1024]{1,0:T(8,128)(2,1)} %refs_7_.1) | copy-start | bytes 12582916
  15.8 31.9 %copy-start.1 = (s32[1,64]{1,0:T(1,128)S(1)}, s32[1,64]{1,0:T(1,128)}, u32[]{:S(2)}) copy-start(s32[1,64]{1,0:T(1,128)} %refs_1_.5) | copy-start | bytes 772
  18.4 11.2 %collective-permute-start.6 = (f32[64,1024]{1,0:T(8,128)S(1)}, f32[64,1024]{1,0:T(8,128)S(1)}, u32[]{:S(2)}, u32[]{:S(2)}) collective-permute-start(f32[64,1024]{1,0:T(8,128)S(1)} %get-tuple-element.28), channel_id=1, source_target_pairs={{1,0},{0,1},{3,2},{2,3},{5,4},{4,5},{7,6},{6,7},{9,8},{8,9},{11,10... | collective-permute-start | bytes 786440 | tf_op jit(solution)/shard_map/ppermute | solution.py:353
  19.5 12.4 %collective-permute-start.7 = (f32[64,1024]{1,0:T(8,128)S(1)}, f32[64,1024]{1,0:T(8,128)S(1)}, u32[]{:S(2)}, u32[]{:S(2)}) collective-permute-start(f32[64,1024]{1,0:T(8,128)S(1)} %get-tuple-element.29), channel_id=1, source_target_pairs={{2,0},{3,1},{0,2},{1,3},{6,4},{7,5},{4,6},{5,7},{10,8},{11,9},{8,1... | collective-permute-start | bytes 786440 | tf_op jit(solution)/shard_map/ppermute | solution.py:353
  20.5 13.1 %collective-permute-start.8 = (f32[64,1024]{1,0:T(8,128)S(1)}, f32[64,1024]{1,0:T(8,128)S(1)}, u32[]{:S(2)}, u32[]{:S(2)}) collective-permute-start(f32[64,1024]{1,0:T(8,128)S(1)} %get-tuple-element.30), channel_id=1, source_target_pairs={{3,0},{2,1},{1,2},{0,3},{7,4},{6,5},{5,6},{4,7},{11,8},{10,9},{9,1... | collective-permute-start | bytes 786440 | tf_op jit(solution)/shard_map/ppermute | solution.py:353
  22.0 14.0 %collective-permute-start.13 = (bf16[2,512,128]{2,1,0:T(8,128)(2,1)S(1)}, bf16[2,512,128]{2,1,0:T(8,128)(2,1)S(1)}, u32[]{:S(2)}, u32[]{:S(2)}) collective-permute-start(bf16[2,512,128]{2,1,0:T(8,128)(2,1)S(1)} %get-tuple-element.35), channel_id=1, source_target_pairs={{0,8},{4,12},{8,24},{12,28},{16,0},{20,4},{24,16},{28,20},{1,9},{5... | collective-permute-start | bytes 786440 | tf_op jit(solution)/shard_map/ppermute | solution.py:345
  25.2 13.1 %collective-permute-start.14 = (bf16[2,512,128]{2,1,0:T(8,128)(2,1)S(1)}, bf16[2,512,128]{2,1,0:T(8,128)(2,1)S(1)}, u32[]{:S(2)}, u32[]{:S(2)}) collective-permute-start(bf16[2,512,128]{2,1,0:T(8,128)(2,1)S(1)} %get-tuple-element.36), channel_id=1, source_target_pairs={{0,24},{4,28},{8,8},{12,12},{16,16},{20,20},{24,0},{28,4},{1,25},{... | collective-permute-start | bytes 786440 | tf_op jit(solution)/shard_map/ppermute | solution.py:345
  29.6 14.4 %collective-permute-start.15 = (bf16[2,512,128]{2,1,0:T(8,128)(2,1)S(1)}, bf16[2,512,128]{2,1,0:T(8,128)(2,1)S(1)}, u32[]{:S(2)}, u32[]{:S(2)}) collective-permute-start(bf16[2,512,128]{2,1,0:T(8,128)(2,1)S(1)} %get-tuple-element.37), channel_id=1, source_target_pairs={{0,12},{4,8},{8,28},{12,24},{16,4},{20,0},{24,20},{28,16},{1,13},{... | collective-permute-start | bytes 786440 | tf_op jit(solution)/shard_map/ppermute | solution.py:345
  31.9 15.8 %collective-permute-start.16 = (bf16[2,512,128]{2,1,0:T(8,128)(2,1)S(1)}, bf16[2,512,128]{2,1,0:T(8,128)(2,1)S(1)}, u32[]{:S(2)}, u32[]{:S(2)}) collective-permute-start(bf16[2,512,128]{2,1,0:T(8,128)(2,1)S(1)} %get-tuple-element.38), channel_id=1, source_target_pairs={{0,28},{4,24},{8,12},{12,8},{16,20},{20,16},{24,4},{28,0},{1,29},{... | collective-permute-start | bytes 786440 | tf_op jit(solution)/shard_map/ppermute | solution.py:345
  33.7 14.0 %collective-permute-start.12 = (bf16[512,128]{1,0:T(8,128)(2,1)S(1)}, bf16[512,128]{1,0:T(8,128)(2,1)S(1)}, u32[]{:S(2)}, u32[]{:S(2)}) collective-permute-start(bf16[512,128]{1,0:T(8,128)(2,1)S(1)} %round_query.1.refs_2_), channel_id=1, source_target_pairs={{0,4},{4,0},{8,16},{12,20},{16,8},{20,12},{24,28},{28,24},{1,5},{5... | collective-permute-start | bytes 393224 | tf_op jit(solution)/shard_map/ppermute | solution.py:357
  35.9 16.3 %collective-permute-start.10 = (bf16[2,512,128]{2,1,0:T(8,128)(2,1)S(1)}, bf16[2,512,128]{2,1,0:T(8,128)(2,1)S(1)}, u32[]{:S(2)}, u32[]{:S(2)}) collective-permute-start(bf16[2,512,128]{2,1,0:T(8,128)(2,1)S(1)} %get-tuple-element.33), channel_id=1, source_target_pairs={{0,4},{4,0},{8,12},{12,8},{16,20},{20,16},{24,28},{28,24},{1,5},{5... | collective-permute-start | bytes 786440 | tf_op jit(solution)/shard_map/ppermute | solution.py:345
  38.3 15.9 %collective-permute-start.11 = (bf16[2,512,128]{2,1,0:T(8,128)(2,1)S(1)}, bf16[2,512,128]{2,1,0:T(8,128)(2,1)S(1)}, u32[]{:S(2)}, u32[]{:S(2)}) collective-permute-start(bf16[2,512,128]{2,1,0:T(8,128)(2,1)S(1)} %get-tuple-element.34), channel_id=1, source_target_pairs={{0,8},{4,12},{8,0},{12,4},{16,24},{20,28},{24,16},{28,20},{1,9},{5... | collective-permute-start | bytes 786440 | tf_op jit(solution)/shard_map/ppermute | solution.py:345
  44.0 15.7 %collective-permute-start.9 = (bf16[2,512,128]{2,1,0:T(8,128)(2,1)S(1)}, bf16[2,512,128]{2,1,0:T(8,128)(2,1)S(1)}, u32[]{:S(2)}, u32[]{:S(2)}) collective-permute-start(bf16[2,512,128]{2,1,0:T(8,128)(2,1)S(1)} %get-tuple-element.31), channel_id=1, source_target_pairs={{0,12},{4,8},{8,4},{12,0},{16,28},{20,24},{24,20},{28,16},{1,13},{... | collective-permute-start | bytes 786440 | tf_op jit(solution)/shard_map/ppermute | solution.py:345
  50.3 10.4 %collective-permute-start.17 = (bf16[144,512]{1,0:T(8,128)(2,1)S(1)}, bf16[144,512]{1,0:T(8,128)(2,1)S(1)}, u32[]{:S(2)}, u32[]{:S(2)}) collective-permute-start(bf16[144,512]{1,0:T(8,128)(2,1)S(1)} %get-tuple-element.40), channel_id=1, source_target_pairs={{0,4},{4,0},{8,16},{12,20},{16,8},{20,12},{24,28},{28,24},{1,5},{5... | collective-permute-start | bytes 442376 | tf_op jit(solution)/shard_map/ppermute | solution.py:366
where the time goes:
time: 61.9 us; the launch traced here: 61.6 us
  waiting for transfers between devices  27.6 us (45%)
  starting transfers between devices  18.9 us (31%)
  Pallas kernels  12.2 us (20%)
  local copies, waits for them, and re-layouts  2.19 us (4%)
  between operations  0.76 us (1%)
    ppermute x7, waiting for transfers between devices, own_heads(): moved[step] = lax.ppermute(block, 'seq', to)  16.5 us
    ppermute x3, waiting for transfers between devices, own_heads(): halves.append(lax.ppermute(blocks[step], 'batch', peers(batch_count, step)))  6.23 us
    ppermute x7, starting transfers between devices, own_heads(): moved[step] = lax.ppermute(block, 'seq', to)  6.22 us
    pallas_call x3, Pallas kernels, attend(): pl.pallas_call(kernel, out_shape=[jax.ShapeDtypeStruct((HD + 16, columns)...  5.58 us
    ppermute x3, starting transfers between devices, own_heads(): halves.append(lax.ppermute(blocks[step], 'batch', peers(batch_count, step)))  4.57 us
    ppermute x3, waiting for transfers between devices, own_heads(): lax.ppermute(partials[step], 'batch', [(b, a) for a, b in peers(batch_cou...  3.87 us
    ppermute x3, starting transfers between devices, own_heads(): lax.ppermute(partials[step], 'batch', [(b, a) for a, b in peers(batch_cou...  3.55 us
    pallas_call x2, Pallas kernels, pack(): pl.pallas_call(kernel, out_shape=shapes, in_specs=[HBM] * len(sources), o...  2.93 us
  transfers between devices with their start and end apart: 18, of which 11 were waited for; matrix products, arithmetic and copies ran while one was open for 0% of the time, Pallas kernels for 12%

commit v1 on v0

--- a/solution.py
+++ b/solution.py
@@ -98,28 +98,23 @@
 
     def kernel(*refs):
         ins, w_ref, outs, stacked = refs[: 2 * count - 1], refs[2 * count - 1], refs[2 * count : -1], refs[-1]
-
-        @pl.when(pl.program_id(0) == 0)
-        def _():
-            mine = lax.rem(lax.axis_index("seq"), 2)
-            stacked[:rows, :] = ins[0][...]
-            for n in range(1, count):
-                for which, ref in ((mine, ins[n]), (1 - mine, ins[count - 1 + n])):
-                    start = pl.multiple_of(which * (depth // 2), HD)
-                    stacked[n * rows : (n + 1) * rows, pl.ds(start, depth // 2)] = ref[...]
-
-        product = jnp.dot(stacked[...], w_ref[...], preferred_element_type=jnp.float32)
-        for n in range(count):
-            outs[n][...] = product[n * rows : (n + 1) * rows]
+        mine = lax.rem(lax.axis_index("seq"), 2)
+        stacked[:rows, :] = ins[0][...]
+        for n in range(1, count):
+            for which, ref in ((mine, ins[n]), (1 - mine, ins[count - 1 + n])):
+                start = pl.multiple_of(which * (depth // 2), HD)
+                stacked[n * rows : (n + 1) * rows, pl.ds(start, depth // 2)] = ref[...]
+        for j in range(0, columns, tile):
+            part = slice(j, j + tile)
+            product = jnp.dot(stacked[...], w_ref[:, part], preferred_element_type=jnp.float32)
+            for n in range(count):
+                outs[n][:, part] = product[n * rows : (n + 1) * rows]
 
     return pl.pallas_call(
         kernel,
-        grid=(columns // tile,),
         out_shape=[jax.ShapeDtypeStruct((rows, columns), jnp.float32)] * count,
-        in_specs=[pl.BlockSpec((rows, depth), lambda j: (0, 0))]
-        + [pl.BlockSpec((rows, depth // 2), lambda j: (0, 0))] * (2 * count - 2)
-        + [pl.BlockSpec((depth, tile), lambda j: (0, j))],
-        out_specs=[pl.BlockSpec((rows, tile), lambda j: (0, j))] * count,
+        in_specs=[VMEM] * (2 * count),
+        out_specs=[VMEM] * count,
         scratch_shapes=[pltpu.VMEM((count * rows, depth), own.dtype)],
         cost_estimate=pl.CostEstimate(
             flops=2 * count * rows * depth * columns,
@@ -143,12 +138,7 @@
     group = width // HD
 
     def kernel(*refs):
-        ins, out, held, sem = refs[: len(partials)], refs[len(partials)], refs[len(partials) + 1 : -1], refs[-1]
-        copies = [pltpu.make_async_copy(src, dst, sem.at[n]) for n, (src, dst) in enumerate(zip(ins, held))]
-        for copy in copies:
-            copy.start()
-        for copy in copies:
-            copy.wait()
+        held, out = refs[:-1], refs[-1]
         for h in range(group):
             head = slice(h * HD, (h + 1) * HD)
             total = held[0][:, head]
@@ -159,10 +149,8 @@
     return pl.pallas_call(
         kernel,
         out_shape=jax.ShapeDtypeStruct((group * tokens, HD), jnp.bfloat16),
-        in_specs=[ANY] * len(partials),
+        in_specs=[VMEM] * len(partials),
         out_specs=VMEM,
-        scratch_shapes=[pltpu.VMEM(x.shape, x.dtype) for x in partials]
-        + [pltpu.SemaphoreType.DMA((len(partials),))],
         cost_estimate=pl.CostEstimate(
             flops=len(partials) * tokens * width,
             transcendentals=0,
@@ -208,25 +196,15 @@
         lengths_ref, positions_ref = refs[:2]
         moved_refs = refs[2 : 2 + len(moved)]
         out = refs[len(inputs)]
-        held = refs[len(inputs) + 1 + send : -1]
-        sem = refs[-1]
-        copies = [
-            pltpu.make_async_copy(src, dst, sem.at[n]) for n, (src, dst) in enumerate(zip(moved_refs, held))
-        ]
-        for copy in copies:
-            copy.start()
+        held = moved_refs
         me = lax.axis_index("seq")
         other = swapped(me, pairs)
         limit = jnp.minimum(positions_ref[...], lengths_ref[0] - 1)
         limit = jnp.concatenate([limit] * (columns // tokens), axis=1)
         rows = lax.broadcasted_iota(jnp.int32, (keys_here, columns), 0)
-        for copy in copies[:n_query]:
-            copy.wait()
         q = held[0][...]
         if n_query == 2:
             q = jnp.where(other == me, q, held[1][...])
-        for copy in copies[n_query:]:
-            copy.wait()
         wide, deep = min(columns, 256), min(keys_here, 128)
         for c in range(0, columns, wide):
             part = slice(c, c + wide)
@@ -274,10 +252,8 @@
         out_shape=[
             jax.ShapeDtypeStruct((HD + 16, columns), dtype) for dtype in (jnp.float32, jnp.bfloat16)[: 1 + send]
         ],
-        in_specs=[SMEM, VMEM] + [ANY] * len(moved) + [VMEM] * (len(inputs) - 2 - len(moved)),
+        in_specs=[SMEM] + [VMEM] * (len(inputs) - 1),
         out_specs=[VMEM] * (1 + send),
-        scratch_shapes=[pltpu.VMEM(x.shape, x.dtype) for x in moved]
-        + [pltpu.SemaphoreType.DMA((len(moved),))],
         cost_estimate=pl.CostEstimate(
             flops=4 * n_chunks * keys_here * columns * HD,
             transcendentals=n_chunks * keys_here * columns,
@@ -292,23 +268,37 @@
     columns = near.shape[1]
     group = columns // tokens
 
-    def kernel(near_ref, far_ref, received_ref, out):
+    def kernel(near_ref, far_ref, received_ref, out, held, sem):
         me = lax.axis_index("seq")
         mine = swapped(me, pairs) == me
-        far_sums = [
-            jnp.where(mine, one, two) for one, two in zip(read_state(far_ref), read_state(received_ref))
-        ]
-        _, denom, numer = merge(*read_state(near_ref), *far_sums)
-        result = numer / denom
-        for h in range(group):
-            part = result[:, h * tokens : (h + 1) * tokens]
-            out[:, h * HD : (h + 1) * HD] = jnp.transpose(part).astype(jnp.bfloat16)
+        wide = 2 * tokens
+        copies = []
+        for n in range(0, group, 2):
+            part = slice(n * tokens, n * tokens + wide)
+            far_sums = [
+                jnp.where(mine, one, two)
+                for one, two in zip(read_state(far_ref, part), read_state(received_ref, part))
+            ]
+            _, denom, numer = merge(*read_state(near_ref, part), *far_sums)
+            result = jnp.transpose(numer * (1.0 / denom)).astype(jnp.bfloat16)
+            for h in range(2):
+                held[:, (n + h) * HD : (n + h + 1) * HD] = result[h * tokens : (h + 1) * tokens]
+            columns_here = slice(n * HD, (n + 2) * HD)
+            copy = pltpu.make_async_copy(held.at[:, columns_here], out.at[:, columns_here], sem.at[n // 2])
+            copy.start()
+            copies.append(copy)
+        for copy in copies:
+            copy.wait()
 
     return pl.pallas_call(
         kernel,
         out_shape=jax.ShapeDtypeStruct((tokens, group * HD), jnp.bfloat16),
         in_specs=[VMEM] * 3,
-        out_specs=VMEM,
+        out_specs=HBM,
+        scratch_shapes=[
+            pltpu.VMEM((tokens, group * HD), jnp.bfloat16),
+            pltpu.SemaphoreType.DMA((group // 2,)),
+        ],
         cost_estimate=pl.CostEstimate(
             flops=8 * HD * columns, transcendentals=0, bytes_accessed=12 * HD * columns
         ),

time: 61.9 us -> 60.2 us (0.973)
  Pallas kernels: 12.2 us -> 9.63 us
  waiting for transfers between devices: 27.6 us -> 28.6 us
    pallas_call x1, Pallas kernels: 2.6 us -> 1.25 us  [project(): pl.pallas_call(kernel, out_shape=[jax.ShapeDtypeStruct((rows, columns), j...]
    pallas_call x3, Pallas kernels: 5.58 us -> 4.53 us  [attend(): pl.pallas_call(kernel, out_shape=[jax.ShapeDtypeStruct((HD + 16, columns)...]
    ppermute x7, waiting for transfers between devices: 16.5 us -> 17.4 us  [own_heads(): moved[step] = lax.ppermute(block, 'seq', to)]
  transfers between devices with their start and end apart: 18 -> 18, of which waited for: 11 -> 11; matrix products, arithmetic and copies ran while one was open for 0% -> 0% of each run, Pallas kernels for 12% -> 10%
where the time goes in v1:
time: 60.2 us; the launch traced here: 60 us
  waiting for transfers between devices  28.6 us (48%)
  starting transfers between devices  18.8 us (31%)
  Pallas kernels  9.63 us (16%)
  local copies, waits for them, and re-layouts  2.19 us (4%)
  between operations  0.75 us (1%)
    ppermute x7, waiting for transfers between devices, own_heads(): moved[step] = lax.ppermute(block, 'seq', to)  17.4 us
    ppermute x3, waiting for transfers between devices, own_heads(): halves.append(lax.ppermute(blocks[step], 'batch', peers(batch_count, step)))  6.23 us
    ppermute x7, starting transfers between devices, own_heads(): moved[step] = lax.ppermute(block, 'seq', to)  6.22 us
    ppermute x3, starting transfers between devices, own_heads(): halves.append(lax.ppermute(blocks[step], 'batch', peers(batch_count, step)))  4.57 us
    pallas_call x3, Pallas kernels, attend(): pl.pallas_call(kernel, out_shape=[jax.ShapeDtypeStruct((HD + 16, columns)...  4.53 us
    ppermute x3, waiting for transfers between devices, own_heads(): lax.ppermute(partials[step], 'batch', [(b, a) for a, b in peers(batch_cou...  3.87 us
    ppermute x3, starting transfers between devices, own_heads(): lax.ppermute(partials[step], 'batch', [(b, a) for a, b in peers(batch_cou...  3.55 us
    pallas_call x2, Pallas kernels, pack(): pl.pallas_call(kernel, out_shape=shapes, in_specs=[HBM] * len(sources), o...  2.93 us
  transfers between devices with their start and end apart: 18, of which 11 were waited for; matrix products, arithmetic and copies ran while one was open for 0% of the time, Pallas kernels for 10%

profile of v1, /device:TPU:0, one launch (start us, length us, event | category | flops | bytes accessed | tf_op | source)
XLA Modules:
  0.0 60.0 jit_solution(15004881464880201851)
XLA Ops:
  0.0 1.2 %shard_map.64 = (bf16[2,512,128]{2,1,0:T(8,128)(2,1)S(1)}, bf16[64,2048]{1,0:T(8,128)(2,1)S(1)}, bf16[64,1024]{1,0:T(8,128)(2,1)S(1)}, bf16[64,1024]{1,0:T(8,128)(2,1)S(1)}, bf16[64,1024]{1,0:T(8,128)(2,1)S(1)}) custom-call(bf16[512,1024]{1,0:T(8,128)(2,1)} %bitcast.4, bf16[512,1024]{1,0:T(8,128)(2,1)} %bitcast.6, bf16[64,8192]{1,0:T(8,128)(2,1)} %bitcast.8), custom_call_target="tpu_custom_call" | custom-call | bytes 524288 | tf_op jit(solution)/shard_map/pallas_call | solution.py:79
  1.3 3.0 %collective-permute-start = (bf16[64,1024]{1,0:T(8,128)(2,1)S(1)}, bf16[64,1024]{1,0:T(8,128)(2,1)S(1)}, u32[]{:S(2)}, u32[]{:S(2)}) collective-permute-start(bf16[64,1024]{1,0:T(8,128)(2,1)S(1)} %get-tuple-element.24), channel_id=1, source_target_pairs={{0,1},{1,0},{2,3},{3,2},{4,5},{5,4},{6,7},{7,6},{8,9},{9,8},{10,11... | collective-permute-start | bytes 393224 | tf_op jit(solution)/shard_map/ppermute | solution.py:338
  4.3 1.5 %collective-permute-start.1 = (bf16[64,1024]{1,0:T(8,128)(2,1)S(1)}, bf16[64,1024]{1,0:T(8,128)(2,1)S(1)}, u32[]{:S(2)}, u32[]{:S(2)}) collective-permute-start(bf16[64,1024]{1,0:T(8,128)(2,1)S(1)} %get-tuple-element.25), channel_id=1, source_target_pairs={{0,2},{1,3},{2,0},{3,1},{4,6},{5,7},{6,4},{7,5},{8,10},{9,11},{10,... | collective-permute-start | bytes 393224 | tf_op jit(solution)/shard_map/ppermute | solution.py:338
  5.8 2.3 %collective-permute-done.refs_1_ = bf16[64,1024]{1,0:T(8,128)(2,1)S(1)} collective-permute-done((bf16[64,1024]{1,0:T(8,128)(2,1)S(1)}, bf16[64,1024]{1,0:T(8,128)(2,1)S(1)}, u32[]{:S(2)}, u32[]{:S(2)}) %collective-permute-start) | collective-permute-done | bytes 131104 | tf_op jit(solution)/shard_map/ppermute | solution.py:338
  8.2 3.9 %collective-permute-done.1.refs_2_ = bf16[64,1024]{1,0:T(8,128)(2,1)S(1)} collective-permute-done((bf16[64,1024]{1,0:T(8,128)(2,1)S(1)}, bf16[64,1024]{1,0:T(8,128)(2,1)S(1)}, u32[]{:S(2)}, u32[]{:S(2)}) %collective-permute-start.1) | collective-permute-done | bytes 131104 | tf_op jit(solution)/shard_map/ppermute | solution.py:338
  12.1 0.5 collective-permute-start.5
  12.6 0.8 %collective-permute-done.4.refs_5_ = bf16[64,1024]{1,0:T(8,128)(2,1)S(1)} collective-permute-done((bf16[64,1024]{1,0:T(8,128)(2,1)S(1)}, bf16[64,1024]{1,0:T(8,128)(2,1)S(1)}, u32[]{:S(2)}, u32[]{:S(2)}) %collective-permute-start.4) | collective-permute-done | bytes 131104 | tf_op jit(solution)/shard_map/ppermute | solution.py:339
  13.4 0.2 collective-permute-done.5.refs_6_
  13.6 2.2 %copy-done = bf16[2048,1024]{1,0:T(8,128)(2,1)S(1)} copy-done((bf16[2048,1024]{1,0:T(8,128)(2,1)S(1)}, bf16[2048,1024]{1,0:T(8,128)(2,1)}, u32[]{:S(2)}) %copy-start) | copy-done | bytes 4194328
  15.8 1.3 %project.1 = (f32[64,1024]{1,0:T(8,128)S(1)}, f32[64,1024]{1,0:T(8,128)S(1)}, f32[64,1024]{1,0:T(8,128)S(1)}, f32[64,1024]{1,0:T(8,128)S(1)}) custom-call(bf16[64,2048]{1,0:T(8,128)(2,1)S(1)} %get-tuple-element.23.refs_0_, bf16[64,1024]{1,0:T(8,128)(2,1)S(1)} %collective-permute-done.refs_1_, bf16[64,1024]{1,0:T(8,128)(2,1)S(1)} %collective-permute-done.1.refs_2_, ...), custom_call_target="tpu_custom_call" | custom-call | flops 1073741824 | bytes 7340032 | tf_op jit(solution)/shard_map/project/pallas_call | solution.py:113
  17.1 1.1 %collective-permute-start.6 = (f32[64,1024]{1,0:T(8,128)S(1)}, f32[64,1024]{1,0:T(8,128)S(1)}, u32[]{:S(2)}, u32[]{:S(2)}) collective-permute-start(f32[64,1024]{1,0:T(8,128)S(1)} %get-tuple-element.28), channel_id=1, source_target_pairs={{1,0},{0,1},{3,2},{2,3},{5,4},{4,5},{7,6},{6,7},{9,8},{8,9},{11,10... | collective-permute-start | bytes 786440 | tf_op jit(solution)/shard_map/ppermute | solution.py:343
  18.2 1.0 %collective-permute-start.7 = (f32[64,1024]{1,0:T(8,128)S(1)}, f32[64,1024]{1,0:T(8,128)S(1)}, u32[]{:S(2)}, u32[]{:S(2)}) collective-permute-start(f32[64,1024]{1,0:T(8,128)S(1)} %get-tuple-element.29), channel_id=1, source_target_pairs={{2,0},{3,1},{0,2},{1,3},{6,4},{7,5},{4,6},{5,7},{10,8},{11,9},{8,1... | collective-permute-start | bytes 786440 | tf_op jit(solution)/shard_map/ppermute | solution.py:343
  19.2 1.4 %collective-permute-start.8 = (f32[64,1024]{1,0:T(8,128)S(1)}, f32[64,1024]{1,0:T(8,128)S(1)}, u32[]{:S(2)}, u32[]{:S(2)}) collective-permute-start(f32[64,1024]{1,0:T(8,128)S(1)} %get-tuple-element.30), channel_id=1, source_target_pairs={{3,0},{2,1},{1,2},{0,3},{7,4},{6,5},{5,6},{4,7},{11,8},{10,9},{9,1... | collective-permute-start | bytes 786440 | tf_op jit(solution)/shard_map/ppermute | solution.py:343
  20.6 1.6 %collective-permute-start.13 = (bf16[2,512,128]{2,1,0:T(8,128)(2,1)S(1)}, bf16[2,512,128]{2,1,0:T(8,128)(2,1)S(1)}, u32[]{:S(2)}, u32[]{:S(2)}) collective-permute-start(bf16[2,512,128]{2,1,0:T(8,128)(2,1)S(1)} %get-tuple-element.35), channel_id=1, source_target_pairs={{0,8},{4,12},{8,24},{12,28},{16,0},{20,4},{24,16},{28,20},{1,9},{5... | collective-permute-start | bytes 786440 | tf_op jit(solution)/shard_map/ppermute | solution.py:335
  22.2 1.7 %shard_map.65 = (bf16[2,512,128]{2,1,0:T(8,128)(2,1)S(1)}, bf16[2,512,128]{2,1,0:T(8,128)(2,1)S(1)}, bf16[2,512,128]{2,1,0:T(8,128)(2,1)S(1)}, bf16[2,512,128]{2...) custom-call(bf16[512,1024]{1,0:T(8,128)(2,1)} %bitcast.5, ...), custom_call_target="tpu_custom_call" | custom-call | bytes 3670016 | tf_op jit(solution)/shard_map/pallas_call | solution.py:79
  23.9 4.4 %collective-permute-start.14 = (bf16[2,512,128]{2,1,0:T(8,128)(2,1)S(1)}, bf16[2,512,128]{2,1,0:T(8,128)(2,1)S(1)}, u32[]{:S(2)}, u32[]{:S(2)}) collective-permute-start(bf16[2,512,128]{2,1,0:T(8,128)(2,1)S(1)} %get-tuple-element.36), channel_id=1, source_target_pairs={{0,24},{4,28},{8,8},{12,12},{16,16},{20,20},{24,0},{28,4},{1,25},{... | collective-permute-start | bytes 786440 | tf_op jit(solution)/shard_map/ppermute | solution.py:335
  28.3 2.2 %collective-permute-done.7.refs_2_ = f32[64,1024]{1,0:T(8,128)S(1)} collective-permute-done((f32[64,1024]{1,0:T(8,128)S(1)}, f32[64,1024]{1,0:T(8,128)S(1)}, u32[]{:S(2)}, u32[]{:S(2)}) %collective-permute-start.7) | collective-permute-done | bytes 262176 | tf_op jit(solution)/shard_map/ppermute | solution.py:343
  30.6 1.6 %collective-permute-done.8.refs_3_ = f32[64,1024]{1,0:T(8,128)S(1)} collective-permute-done((f32[64,1024]{1,0:T(8,128)S(1)}, f32[64,1024]{1,0:T(8,128)S(1)}, u32[]{:S(2)}, u32[]{:S(2)}) %collective-permute-start.8) | collective-permute-done | bytes 262176 | tf_op jit(solution)/shard_map/ppermute | solution.py:343
  32.2 0.1 round_query.1.refs_2_
  32.3 2.2 %collective-permute-start.12 = (bf16[512,128]{1,0:T(8,128)(2,1)S(1)}, bf16[512,128]{1,0:T(8,128)(2,1)S(1)}, u32[]{:S(2)}, u32[]{:S(2)}) collective-permute-start(bf16[512,128]{1,0:T(8,128)(2,1)S(1)} %round_query.1.refs_2_), channel_id=1, source_target_pairs={{0,4},{4,0},{8,16},{12,20},{16,8},{20,12},{24,28},{28,24},{1,5},{5... | collective-permute-start | bytes 393224 | tf_op jit(solution)/shard_map/ppermute | solution.py:347
  34.4 0.1 collective-permute-start.10
  34.5 2.4 %collective-permute-done.14.refs_5_ = bf16[2,512,128]{2,1,0:T(8,128)(2,1)S(1)} collective-permute-done((bf16[2,512,128]{2,1,0:T(8,128)(2,1)S(1)}, bf16[2,512,128]{2,1,0:T(8,128)(2,1)S(1)}, u32[]{:S(2)}, u32[]{:S(2)}) %collective-permute-start.14) | collective-permute-done | bytes 262176 | tf_op jit(solution)/shard_map/ppermute | solution.py:335
  36.9 5.7 %collective-permute-done.15.refs_6_ = bf16[2,512,128]{2,1,0:T(8,128)(2,1)S(1)} collective-permute-done((bf16[2,512,128]{2,1,0:T(8,128)(2,1)S(1)}, bf16[2,512,128]{2,1,0:T(8,128)(2,1)S(1)}, u32[]{:S(2)}, u32[]{:S(2)}) %collective-permute-start.15) | collective-permute-done | bytes 262176 | tf_op jit(solution)/shard_map/ppermute | solution.py:335
  42.7 0.1 collective-permute-start.9
  43.4 2.9 %collective-permute-done.16.refs_7_ = bf16[2,512,128]{2,1,0:T(8,128)(2,1)S(1)} collective-permute-done((bf16[2,512,128]{2,1,0:T(8,128)(2,1)S(1)}, bf16[2,512,128]{2,1,0:T(8,128)(2,1)S(1)}, u32[]{:S(2)}, u32[]{:S(2)}) %collective-permute-start.16) | collective-permute-done | bytes 262176 | tf_op jit(solution)/shard_map/ppermute | solution.py:335
  46.4 2.1 %attend.5 = (f32[144,512]{1,0:T(8,128)S(1)}, bf16[144,512]{1,0:T(8,128)(2,1)S(1)}) custom-call(s32[1]{0:T(128)S(6)} %copy.7.refs_0_, s32[1,64]{1,0:T(1,128)S(1)} %copy-done.1, bf16[512,128]{1,0:T(8,128)(2,1)S(1)} %round_query.1.refs_2_, bf16[512,128]{1,0:T(8,128)(2,1)S(1)} %collective-permute-done.12.refs_3_, ...), custom_call_target="tpu_custom_call" | custom-call | flops 536870912 | bytes 1048576 | tf_op jit(solution)/shard_map/attend/pallas_call | solution.py:250
  48.5 1.8 %collective-permute-start.17 = (bf16[144,512]{1,0:T(8,128)(2,1)S(1)}, bf16[144,512]{1,0:T(8,128)(2,1)S(1)}, u32[]{:S(2)}, u32[]{:S(2)}) collective-permute-start(bf16[144,512]{1,0:T(8,128)(2,1)S(1)} %get-tuple-element.40), channel_id=1, source_target_pairs={{0,4},{4,0},{8,16},{12,20},{16,8},{20,12},{24,28},{28,24},{1,5},{5... | collective-permute-start | bytes 442376 | tf_op jit(solution)/shard_map/ppermute | solution.py:356
  50.3 2.6 %collective-permute-done.11.refs_5_ = bf16[2,512,128]{2,1,0:T(8,128)(2,1)S(1)} collective-permute-done((bf16[2,512,128]{2,1,0:T(8,128)(2,1)S(1)}, bf16[2,512,128]{2,1,0:T(8,128)(2,1)S(1)}, u32[]{:S(2)}, u32[]{:S(2)}) %collective-permute-start.11) | collective-permute-done | bytes 262176 | tf_op jit(solution)/shard_map/ppermute | solution.py:335
  52.9 1.6 %attend.3.refs_4_ = f32[144,512]{1,0:T(8,128)S(1)} custom-call(s32[1]{0:T(128)S(6)} %copy.7.refs_0_, s32[1,64]{1,0:T(1,128)S(1)} %copy-done.1, bf16[512,128]{1,0:T(8,128)(2,1)S(1)} %round_query.1.refs_2_, bf16[2,512,128]{2,1,0:T(8,128)(2,1)S(1)} %get-tuple-element.32.refs_3_, bf16[2,512,128]{2,1,0:T(8,128)(2,1)S(1)} %collective-permute-done.10.refs_4_, ...), custom_call_target="tpu_custom_call" | custom-call | flops 402653184 | bytes 786432 | tf_op jit(solution)/shard_map/attend/pallas_call | solution.py:250
  54.5 3.8 %collective-permute-done.9.refs_3_ = bf16[2,512,128]{2,1,0:T(8,128)(2,1)S(1)} collective-permute-done((bf16[2,512,128]{2,1,0:T(8,128)(2,1)S(1)}, bf16[2,512,128]{2,1,0:T(8,128)(2,1)S(1)}, u32[]{:S(2)}, u32[]{:S(2)}) %collective-permute-start.9) | collective-permute-done | bytes 262176 | tf_op jit(solution)/shard_map/ppermute | solution.py:335
  58.3 0.8 %attend.4.near_ref = f32[144,512]{1,0:T(8,128)S(1)} custom-call(s32[1]{0:T(128)S(6)} %copy.7.refs_0_, s32[1,64]{1,0:T(1,128)S(1)} %copy-done.1, bf16[512,128]{1,0:T(8,128)(2,1)S(1)} %round_query.1.refs_2_, bf16[2,512,128]{2,1,0:T(8,128)(2,1)S(1)} %collective-permute-done.9.refs_3_, f32[144,512]{1,0:T(8,128)S(1)} %attend.3.refs_4_), custom_call_target="tpu_custom_call" | custom-call | flops 134217728 | bytes 262144 | tf_op jit(solution)/shard_map/attend/pallas_call | solution.py:250
  59.1 0.8 %finish.1 = bf16[64,1024]{1,0:T(8,128)(2,1)} custom-call(f32[144,512]{1,0:T(8,128)S(1)} %attend.4.near_ref, f32[144,512]{1,0:T(8,128)S(1)} %get-tuple-element.39.far_ref, bf16[144,512]{1,0:T(8,128)(2,1)S(1)} %collective-permute-done.17.received_ref), custom_call_target="tpu_custom_call" | custom-call | flops 524288 | bytes 786432 | tf_op jit(solution)/shard_map/finish/pallas_call | solution.py:293
  (16 shorter events, 0.1 us)
Async XLA Ops:
  1.3 6.9 %collective-permute-start = (bf16[64,1024]{1,0:T(8,128)(2,1)S(1)}, bf16[64,1024]{1,0:T(8,128)(2,1)S(1)}, u32[]{:S(2)}, u32[]{:S(2)}) collective-permute-start(bf16[64,1024]{1,0:T(8,128)(2,1)S(1)} %get-tuple-element.24), channel_id=1, source_target_pairs={{0,1},{1,0},{2,3},{3,2},{4,5},{5,4},{6,7},{7,6},{8,9},{9,8},{10,11... | collective-permute-start | bytes 393224 | tf_op jit(solution)/shard_map/ppermute | solution.py:338
  4.3 7.8 %collective-permute-start.1 = (bf16[64,1024]{1,0:T(8,128)(2,1)S(1)}, bf16[64,1024]{1,0:T(8,128)(2,1)S(1)}, u32[]{:S(2)}, u32[]{:S(2)}) collective-permute-start(bf16[64,1024]{1,0:T(8,128)(2,1)S(1)} %get-tuple-element.25), channel_id=1, source_target_pairs={{0,2},{1,3},{2,0},{3,1},{4,6},{5,7},{6,4},{7,5},{8,10},{9,11},{10,... | collective-permute-start | bytes 393224 | tf_op jit(solution)/shard_map/ppermute | solution.py:338
  5.8 6.3 %collective-permute-start.2 = (bf16[64,1024]{1,0:T(8,128)(2,1)S(1)}, bf16[64,1024]{1,0:T(8,128)(2,1)S(1)}, u32[]{:S(2)}, u32[]{:S(2)}) collective-permute-start(bf16[64,1024]{1,0:T(8,128)(2,1)S(1)} %get-tuple-element.26), channel_id=1, source_target_pairs={{0,3},{1,2},{2,1},{3,0},{4,7},{5,6},{6,5},{7,4},{8,11},{9,10},{10,... | collective-permute-start | bytes 393224 | tf_op jit(solution)/shard_map/ppermute | solution.py:338
  8.2 4.4 %collective-permute-start.3 = (bf16[64,1024]{1,0:T(8,128)(2,1)S(1)}, bf16[64,1024]{1,0:T(8,128)(2,1)S(1)}, u32[]{:S(2)}, u32[]{:S(2)}) collective-permute-start(bf16[64,1024]{1,0:T(8,128)(2,1)S(1)} %collective-permute-done.refs_1_), channel_id=1, source_target_pairs={{0,4},{4,0},{8,12},{12,8},{16,20},{20,16},{24,28},{28,24},{1,5},{5... | collective-permute-start | bytes 393224 | tf_op jit(solution)/shard_map/ppermute | solution.py:339
  12.1 1.3 %collective-permute-start.4 = (bf16[64,1024]{1,0:T(8,128)(2,1)S(1)}, bf16[64,1024]{1,0:T(8,128)(2,1)S(1)}, u32[]{:S(2)}, u32[]{:S(2)}) collective-permute-start(bf16[64,1024]{1,0:T(8,128)(2,1)S(1)} %collective-permute-done.1.refs_2_), channel_id=1, source_target_pairs={{0,4},{4,0},{8,12},{12,8},{16,20},{20,16},{24,28},{28,24},{1,5},{5... | collective-permute-start | bytes 393224 | tf_op jit(solution)/shard_map/ppermute | solution.py:339
  12.1 1.5 %collective-permute-start.5 = (bf16[64,1024]{1,0:T(8,128)(2,1)S(1)}, bf16[64,1024]{1,0:T(8,128)(2,1)S(1)}, u32[]{:S(2)}, u32[]{:S(2)}) collective-permute-start(bf16[64,1024]{1,0:T(8,128)(2,1)S(1)} %collective-permute-done.2.refs_3_), channel_id=1, source_target_pairs={{0,4},{4,0},{8,12},{12,8},{16,20},{20,16},{24,28},{28,24},{1,5},{5... | collective-permute-start | bytes 393224 | tf_op jit(solution)/shard_map/ppermute | solution.py:339
  13.6 2.2 %copy-start = (bf16[2048,1024]{1,0:T(8,128)(2,1)S(1)}, bf16[2048,1024]{1,0:T(8,128)(2,1)}, u32[]{:S(2)}) copy-start(bf16[2048,1024]{1,0:T(8,128)(2,1)} %refs_7_.1) | copy-start | bytes 12582916
  15.8 30.6 %copy-start.1 = (s32[1,64]{1,0:T(1,128)S(1)}, s32[1,64]{1,0:T(1,128)}, u32[]{:S(2)}) copy-start(s32[1,64]{1,0:T(1,128)} %refs_1_.5) | copy-start | bytes 772
  17.1 11.2 %collective-permute-start.6 = (f32[64,1024]{1,0:T(8,128)S(1)}, f32[64,1024]{1,0:T(8,128)S(1)}, u32[]{:S(2)}, u32[]{:S(2)}) collective-permute-start(f32[64,1024]{1,0:T(8,128)S(1)} %get-tuple-element.28), channel_id=1, source_target_pairs={{1,0},{0,1},{3,2},{2,3},{5,4},{4,5},{7,6},{6,7},{9,8},{8,9},{11,10... | collective-permute-start | bytes 786440 | tf_op jit(solution)/shard_map/ppermute | solution.py:343
  18.2 12.4 %collective-permute-start.7 = (f32[64,1024]{1,0:T(8,128)S(1)}, f32[64,1024]{1,0:T(8,128)S(1)}, u32[]{:S(2)}, u32[]{:S(2)}) collective-permute-start(f32[64,1024]{1,0:T(8,128)S(1)} %get-tuple-element.29), channel_id=1, source_target_pairs={{2,0},{3,1},{0,2},{1,3},{6,4},{7,5},{4,6},{5,7},{10,8},{11,9},{8,1... | collective-permute-start | bytes 786440 | tf_op jit(solution)/shard_map/ppermute | solution.py:343
  19.2 13.1 %collective-permute-start.8 = (f32[64,1024]{1,0:T(8,128)S(1)}, f32[64,1024]{1,0:T(8,128)S(1)}, u32[]{:S(2)}, u32[]{:S(2)}) collective-permute-start(f32[64,1024]{1,0:T(8,128)S(1)} %get-tuple-element.30), channel_id=1, source_target_pairs={{3,0},{2,1},{1,2},{0,3},{7,4},{6,5},{5,6},{4,7},{11,8},{10,9},{9,1... | collective-permute-start | bytes 786440 | tf_op jit(solution)/shard_map/ppermute | solution.py:343
  20.6 13.8 %collective-permute-start.13 = (bf16[2,512,128]{2,1,0:T(8,128)(2,1)S(1)}, bf16[2,512,128]{2,1,0:T(8,128)(2,1)S(1)}, u32[]{:S(2)}, u32[]{:S(2)}) collective-permute-start(bf16[2,512,128]{2,1,0:T(8,128)(2,1)S(1)} %get-tuple-element.35), channel_id=1, source_target_pairs={{0,8},{4,12},{8,24},{12,28},{16,0},{20,4},{24,16},{28,20},{1,9},{5... | collective-permute-start | bytes 786440 | tf_op jit(solution)/shard_map/ppermute | solution.py:335
  23.9 13.1 %collective-permute-start.14 = (bf16[2,512,128]{2,1,0:T(8,128)(2,1)S(1)}, bf16[2,512,128]{2,1,0:T(8,128)(2,1)S(1)}, u32[]{:S(2)}, u32[]{:S(2)}) collective-permute-start(bf16[2,512,128]{2,1,0:T(8,128)(2,1)S(1)} %get-tuple-element.36), channel_id=1, source_target_pairs={{0,24},{4,28},{8,8},{12,12},{16,16},{20,20},{24,0},{28,4},{1,25},{... | collective-permute-start | bytes 786440 | tf_op jit(solution)/shard_map/ppermute | solution.py:335
  28.3 14.4 %collective-permute-start.15 = (bf16[2,512,128]{2,1,0:T(8,128)(2,1)S(1)}, bf16[2,512,128]{2,1,0:T(8,128)(2,1)S(1)}, u32[]{:S(2)}, u32[]{:S(2)}) collective-permute-start(bf16[2,512,128]{2,1,0:T(8,128)(2,1)S(1)} %get-tuple-element.37), channel_id=1, source_target_pairs={{0,12},{4,8},{8,28},{12,24},{16,4},{20,0},{24,20},{28,16},{1,13},{... | collective-permute-start | bytes 786440 | tf_op jit(solution)/shard_map/ppermute | solution.py:335
  30.6 15.8 %collective-permute-start.16 = (bf16[2,512,128]{2,1,0:T(8,128)(2,1)S(1)}, bf16[2,512,128]{2,1,0:T(8,128)(2,1)S(1)}, u32[]{:S(2)}, u32[]{:S(2)}) collective-permute-start(bf16[2,512,128]{2,1,0:T(8,128)(2,1)S(1)} %get-tuple-element.38), channel_id=1, source_target_pairs={{0,28},{4,24},{8,12},{12,8},{16,20},{20,16},{24,4},{28,0},{1,29},{... | collective-permute-start | bytes 786440 | tf_op jit(solution)/shard_map/ppermute | solution.py:335
  32.3 14.1 %collective-permute-start.12 = (bf16[512,128]{1,0:T(8,128)(2,1)S(1)}, bf16[512,128]{1,0:T(8,128)(2,1)S(1)}, u32[]{:S(2)}, u32[]{:S(2)}) collective-permute-start(bf16[512,128]{1,0:T(8,128)(2,1)S(1)} %round_query.1.refs_2_), channel_id=1, source_target_pairs={{0,4},{4,0},{8,16},{12,20},{16,8},{20,12},{24,28},{28,24},{1,5},{5... | collective-permute-start | bytes 393224 | tf_op jit(solution)/shard_map/ppermute | solution.py:347
  34.4 15.9 %collective-permute-start.10 = (bf16[2,512,128]{2,1,0:T(8,128)(2,1)S(1)}, bf16[2,512,128]{2,1,0:T(8,128)(2,1)S(1)}, u32[]{:S(2)}, u32[]{:S(2)}) collective-permute-start(bf16[2,512,128]{2,1,0:T(8,128)(2,1)S(1)} %get-tuple-element.33), channel_id=1, source_target_pairs={{0,4},{4,0},{8,12},{12,8},{16,20},{20,16},{24,28},{28,24},{1,5},{5... | collective-permute-start | bytes 786440 | tf_op jit(solution)/shard_map/ppermute | solution.py:335
  36.9 15.9 %collective-permute-start.11 = (bf16[2,512,128]{2,1,0:T(8,128)(2,1)S(1)}, bf16[2,512,128]{2,1,0:T(8,128)(2,1)S(1)}, u32[]{:S(2)}, u32[]{:S(2)}) collective-permute-start(bf16[2,512,128]{2,1,0:T(8,128)(2,1)S(1)} %get-tuple-element.34), channel_id=1, source_target_pairs={{0,8},{4,12},{8,0},{12,4},{16,24},{20,28},{24,16},{28,20},{1,9},{5... | collective-permute-start | bytes 786440 | tf_op jit(solution)/shard_map/ppermute | solution.py:335
  42.7 15.7 %collective-permute-start.9 = (bf16[2,512,128]{2,1,0:T(8,128)(2,1)S(1)}, bf16[2,512,128]{2,1,0:T(8,128)(2,1)S(1)}, u32[]{:S(2)}, u32[]{:S(2)}) collective-permute-start(bf16[2,512,128]{2,1,0:T(8,128)(2,1)S(1)} %get-tuple-element.31), channel_id=1, source_target_pairs={{0,12},{4,8},{8,4},{12,0},{16,28},{20,24},{24,20},{28,16},{1,13},{... | collective-permute-start | bytes 786440 | tf_op jit(solution)/shard_map/ppermute | solution.py:335
  48.5 10.6 %collective-permute-start.17 = (bf16[144,512]{1,0:T(8,128)(2,1)S(1)}, bf16[144,512]{1,0:T(8,128)(2,1)S(1)}, u32[]{:S(2)}, u32[]{:S(2)}) collective-permute-start(bf16[144,512]{1,0:T(8,128)(2,1)S(1)} %get-tuple-element.40), channel_id=1, source_target_pairs={{0,4},{4,0},{8,16},{12,20},{16,8},{20,12},{24,28},{28,24},{1,5},{5... | collective-permute-start | bytes 442376 | tf_op jit(solution)/shard_map/ppermute | solution.py:356

commit v2 on v1

--- a/solution.py
+++ b/solution.py
@@ -18,6 +18,7 @@
 VMEM = pl.BlockSpec(memory_space=pltpu.VMEM)
 SMEM = pl.BlockSpec(memory_space=pltpu.SMEM)
 PARTNERS = 2
+FIRST = 2
 SMALL = pltpu.CompilerParams(vmem_limit_bytes=24 << 20)
 LOG2E = 1.4426950408889634
 NONE_VISIBLE = -1e30
@@ -39,8 +40,7 @@
 
 def seq_order(count):
     half = count // 2
-    far = [*range(half + 2, count, 2), *range(half + 1, count, 2)]
-    return [half, *range(2, half), *far, 1]
+    return [half, half + 1, *range(half + 2, count), *range(2, half), 1]
 
 
 def pack(key_rows, value_rows, tokens, seq_count, batch_count, steps):
@@ -138,19 +138,20 @@
     group = width // HD
 
     def kernel(*refs):
-        held, out = refs[:-1], refs[-1]
+        held, outs = refs[:-2], refs[-2:]
         for h in range(group):
             head = slice(h * HD, (h + 1) * HD)
             total = held[0][:, head]
             for ref in held[1:]:
                 total = total + ref[:, head]
-            out[h * tokens : (h + 1) * tokens, :] = total.astype(jnp.bfloat16)
+            half, row = divmod(h, group // 2)
+            outs[half][row * tokens : (row + 1) * tokens, :] = total.astype(jnp.bfloat16)
 
     return pl.pallas_call(
         kernel,
-        out_shape=jax.ShapeDtypeStruct((group * tokens, HD), jnp.bfloat16),
+        out_shape=[jax.ShapeDtypeStruct((group // 2 * tokens, HD), jnp.bfloat16)] * 2,
         in_specs=[VMEM] * len(partials),
-        out_specs=VMEM,
+        out_specs=[VMEM] * 2,
         cost_estimate=pl.CostEstimate(
             flops=len(partials) * tokens * width,
             transcendentals=0,
@@ -182,45 +183,40 @@
     return high, middle, x - high - middle
 
 
-def attend(queries, chunks, steps, state, positions, lengths, seq_count, pairs, send=False):
+def attend(own, met, chunks, steps, state, positions, lengths, seq_count, pairs, send=False):
     first = state is None
     tokens = positions.shape[1]
-    columns = queries[0].shape[0]
-    n_query = len(queries)
+    wide = own[0].shape[0]
+    columns = wide * len(own)
     n_chunks = len(chunks)
     keys_here = chunks[0].shape[-2]
-    moved = [*queries, *chunks]
-    inputs = [lengths, positions, *moved] + ([] if first else [state])
+    inputs = [lengths, positions, *own, *met, *chunks] + ([] if first else [state])
 
     def kernel(*refs):
         lengths_ref, positions_ref = refs[:2]
-        moved_refs = refs[2 : 2 + len(moved)]
+        own_refs, rest = refs[2 : 2 + len(own)], refs[2 + len(own) :]
+        met_refs, chunk_refs = rest[: len(met)], rest[len(met) : len(met) + n_chunks]
         out = refs[len(inputs)]
-        held = moved_refs
         me = lax.axis_index("seq")
         other = swapped(me, pairs)
         limit = jnp.minimum(positions_ref[...], lengths_ref[0] - 1)
-        limit = jnp.concatenate([limit] * (columns // tokens), axis=1)
-        rows = lax.broadcasted_iota(jnp.int32, (keys_here, columns), 0)
-        q = held[0][...]
-        if n_query == 2:
-            q = jnp.where(other == me, q, held[1][...])
-        wide, deep = min(columns, 256), min(keys_here, 128)
-        for c in range(0, columns, wide):
-            part = slice(c, c + wide)
+        limit = jnp.concatenate([limit] * (wide // tokens), axis=1)
+        deep = min(keys_here, 128)
+        rows = lax.broadcasted_iota(jnp.int32, (deep, wide), 0)
+        for piece in range(len(own)):
+            q = own_refs[piece][...]
+            if met:
+                q = jnp.where(other == me, q, met_refs[piece][...])
+            part = slice(piece * wide, (piece + 1) * wide)
             sums = None if first else read_state(refs[len(inputs) - 1], part)
-            for n, step in enumerate(steps):
+            for ref, step in zip(chunk_refs, steps):
                 start = source(other, seq_count, step) * keys_here
-                ref = held[n_query + n]
                 scores = []
                 for r in range(0, keys_here, deep):
                     score = lax.dot_general(
-                        ref[0, r : r + deep],
-                        q[part],
-                        (((1,), (1,)), ((), ())),
-                        preferred_element_type=jnp.float32,
+                        ref[0, r : r + deep], q, (((1,), (1,)), ((), ())), preferred_element_type=jnp.float32
                     )
-                    scores.append(jnp.where(rows[:deep, part] <= limit[:, part] - (start + r), score, NONE_VISIBLE))
+                    scores.append(jnp.where(rows <= limit - (start + r), score, NONE_VISIBLE))
                 block_max = functools.reduce(
                     jnp.maximum, [jnp.max(score, axis=0, keepdims=True) for score in scores]
                 )
@@ -268,16 +264,22 @@
     columns = near.shape[1]
     group = columns // tokens
 
-    def kernel(near_ref, far_ref, received_ref, out, held, sem):
+    def kernel(near_ref, *refs):
+        far_refs, received_refs = refs[: len(far)], refs[len(far) : 2 * len(far)]
+        out, held, sem = refs[2 * len(far) :]
         me = lax.axis_index("seq")
         mine = swapped(me, pairs) == me
         wide = 2 * tokens
         copies = []
         for n in range(0, group, 2):
             part = slice(n * tokens, n * tokens + wide)
+            which, start = divmod(n * tokens, far[0].shape[1])
+            inner = slice(start, start + wide)
             far_sums = [
                 jnp.where(mine, one, two)
-                for one, two in zip(read_state(far_ref, part), read_state(received_ref, part))
+                for one, two in zip(
+                    read_state(far_refs[which], inner), read_state(received_refs[which], inner)
+                )
             ]
             _, denom, numer = merge(*read_state(near_ref, part), *far_sums)
             result = jnp.transpose(numer * (1.0 / denom)).astype(jnp.bfloat16)
@@ -293,7 +295,7 @@
     return pl.pallas_call(
         kernel,
         out_shape=jax.ShapeDtypeStruct((tokens, group * HD), jnp.bfloat16),
-        in_specs=[VMEM] * 3,
+        in_specs=[VMEM] * (1 + 2 * len(far)),
         out_specs=HBM,
         scratch_shapes=[
             pltpu.VMEM((tokens, group * HD), jnp.bfloat16),
@@ -304,7 +306,7 @@
         ),
         compiler_params=SMALL,
         name="finish",
-    )(near, far, received)
+    )(near, *far, *received)
 
 
 def partner_pairs(count):
@@ -324,9 +326,9 @@
     key_rows, value_rows, tokens = (
         pltpu.with_memory_space_constraint(x[0], pltpu.HBM) for x in (cache_keys, cache_values, inputs)
     )
-    packed = pack(key_rows, value_rows, tokens, seq_count, batch_count, order[:1])
-    packed, blocks = packed[:1], packed[1:]
-    packed += pack(key_rows, value_rows, None, seq_count, batch_count, [*order[1:], 0])
+    packed = pack(key_rows, value_rows, tokens, seq_count, batch_count, order[:FIRST])
+    packed, blocks = packed[:FIRST], packed[FIRST:]
+    packed += pack(key_rows, value_rows, None, seq_count, batch_count, [*order[FIRST:], 0])
     moved = {0: packed[-1]}
     for step, block in zip(order, packed):
         to = peers(seq_count, step)
@@ -342,19 +344,20 @@
     for step in range(1, batch_count):
         back.append(lax.ppermute(partials[step], "batch", [(b, a) for a, b in peers(batch_count, step)]))
     query = round_query(back)
-    queries = [query]
-    if pairs:
-        queries.append(lax.ppermute(query, "seq", meet))
     attend_ = functools.partial(attend, positions=positions, lengths=lengths, seq_count=seq_count)
     early, far_steps = [*range(half)], [s for s in order if s >= half]
+    far, received = [], []
+    for piece in query:
+        met = lax.ppermute(piece, "seq", meet)
+        sums, sent = attend_(
+            [piece], [met], [moved[s] for s in far_steps], far_steps, None, pairs=pairs, send=True
+        )
+        received.append(lax.ppermute(sent, "seq", meet))
+        far.append(sums)
     near = None
     for steps in (early[:-1], early[-1:]):
-        (near,) = attend_([query], [moved[s] for s in steps], steps, near, pairs=[])
-    far = attend_(queries, [moved[s] for s in far_steps], far_steps, None, pairs=pairs, send=bool(pairs))
-    received = far[0]
-    if pairs:
-        received = lax.ppermute(far[1], "seq", meet)
-    return finish(near, far[0], received, positions.shape[1], pairs)[None]
+        (near,) = attend_(query, [], [moved[s] for s in steps], steps, near, pairs=[])
+    return finish(near, far, received, positions.shape[1], pairs)[None]
 
 
 def split_positions(inputs, w_query, cache_keys, cache_values, lengths, positions):

time: 60.2 us -> 55.3 us (0.919)
  waiting for transfers between devices: 28.6 us -> 21.2 us
  starting transfers between devices: 18.8 us -> 20.9 us
    ppermute x7, waiting for transfers between devices: 17.4 us -> 10.8 us  [own_heads(): moved[step] = lax.ppermute(block, 'seq', to)]
    ppermute x7, starting transfers between devices: 6.22 us -> 9.86 us  [own_heads(): moved[step] = lax.ppermute(block, 'seq', to)]
    ppermute x2 -> x4, starting transfers between devices: 3.98 us -> 2.42 us  [the longest x2 1.8 us: own_heads(): met = lax.ppermute(piece, 'seq', meet)]
    ppermute x3, waiting for transfers between devices: 1.02 us -> 0.01 us  [own_heads(): other_halves.append(lax.ppermute(halves[-1], 'seq', peers(seq_count, 1)))]
    pallas_call x3 -> x4, Pallas kernels: 4.53 us -> 4.91 us  [attend(): pl.pallas_call(kernel, out_shape=[jax.ShapeDtypeStruct((HD + 16, columns)...]
  transfers between devices with their start and end apart: 18 -> 20, of which waited for: 11 -> 8; matrix products, arithmetic and copies ran while one was open for 0% -> 0% of each run, Pallas kernels for 10% -> 14%
where the time goes in v2:
time: 55.3 us; the launch traced here: 55.1 us
  waiting for transfers between devices  21.2 us (38%)
  starting transfers between devices  20.9 us (38%)
  Pallas kernels  9.99 us (18%)
  local copies, waits for them, and re-layouts  2.19 us (4%)
  between operations  0.81 us (1%)
    ppermute x7, waiting for transfers between devices, own_heads(): moved[step] = lax.ppermute(block, 'seq', to)  10.8 us
    ppermute x7, starting transfers between devices, own_heads(): moved[step] = lax.ppermute(block, 'seq', to)  9.86 us
    ppermute x3, waiting for transfers between devices, own_heads(): halves.append(lax.ppermute(blocks[step], 'batch', peers(batch_count, step)))  6.23 us
    pallas_call x4, Pallas kernels, attend(): pl.pallas_call(kernel, out_shape=[jax.ShapeDtypeStruct((HD + 16, columns)...  4.91 us
    ppermute x3, starting transfers between devices, own_heads(): halves.append(lax.ppermute(blocks[step], 'batch', peers(batch_count, step)))  4.57 us
    ppermute x3, waiting for transfers between devices, own_heads(): lax.ppermute(partials[step], 'batch', [(b, a) for a, b in peers(batch_cou...  4.08 us
    ppermute x3, starting transfers between devices, own_heads(): lax.ppermute(partials[step], 'batch', [(b, a) for a, b in peers(batch_cou...  3.55 us
    pallas_call x2, Pallas kernels, pack(): pl.pallas_call(kernel, out_shape=shapes, in_specs=[HBM] * len(sources), o...  2.93 us
  transfers between devices with their start and end apart: 20, of which 8 were waited for; matrix products, arithmetic and copies ran while one was open for 0% of the time, Pallas kernels for 14%

profile of v2, /device:TPU:0, one launch (start us, length us, event | category | flops | bytes accessed | tf_op | source)
XLA Modules:
  0.0 55.1 jit_solution(6540751800935775827)
XLA Ops:
  0.0 1.3 %shard_map.64 = (bf16[2,512,128]{2,1,0:T(8,128)(2,1)S(1)}, bf16[2,512,128]{2,1,0:T(8,128)(2,1)S(1)}, bf16[64,2048]{1,0:T(8,128)(2,1)S(1)}, bf16[64,1024]{1,0:T(8...) custom-call(bf16[512,1024]{1,0:T(8,128)(2,1)} %bitcast.4, bf16[512,1024]{1,0:T(8,128)(2,1)} %bitcast.6, ...), custom_call_target="tpu_custom_call" | custom-call | bytes 1048576 | tf_op jit(solution)/shard_map/pallas_call | solution.py:79
  1.4 3.0 %collective-permute-start = (bf16[64,1024]{1,0:T(8,128)(2,1)S(1)}, bf16[64,1024]{1,0:T(8,128)(2,1)S(1)}, u32[]{:S(2)}, u32[]{:S(2)}) collective-permute-start(bf16[64,1024]{1,0:T(8,128)(2,1)S(1)} %get-tuple-element.28), channel_id=1, source_target_pairs={{0,1},{1,0},{2,3},{3,2},{4,5},{5,4},{6,7},{7,6},{8,9},{9,8},{10,11... | collective-permute-start | bytes 393224 | tf_op jit(solution)/shard_map/ppermute | solution.py:340
  4.4 1.5 %collective-permute-start.1 = (bf16[64,1024]{1,0:T(8,128)(2,1)S(1)}, bf16[64,1024]{1,0:T(8,128)(2,1)S(1)}, u32[]{:S(2)}, u32[]{:S(2)}) collective-permute-start(bf16[64,1024]{1,0:T(8,128)(2,1)S(1)} %get-tuple-element.29), channel_id=1, source_target_pairs={{0,2},{1,3},{2,0},{3,1},{4,6},{5,7},{6,4},{7,5},{8,10},{9,11},{10,... | collective-permute-start | bytes 393224 | tf_op jit(solution)/shard_map/ppermute | solution.py:340
  5.9 2.3 %collective-permute-done.refs_1_ = bf16[64,1024]{1,0:T(8,128)(2,1)S(1)} collective-permute-done((bf16[64,1024]{1,0:T(8,128)(2,1)S(1)}, bf16[64,1024]{1,0:T(8,128)(2,1)S(1)}, u32[]{:S(2)}, u32[]{:S(2)}) %collective-permute-start) | collective-permute-done | bytes 131104 | tf_op jit(solution)/shard_map/ppermute | solution.py:340
  8.3 3.9 %collective-permute-done.1.refs_2_ = bf16[64,1024]{1,0:T(8,128)(2,1)S(1)} collective-permute-done((bf16[64,1024]{1,0:T(8,128)(2,1)S(1)}, bf16[64,1024]{1,0:T(8,128)(2,1)S(1)}, u32[]{:S(2)}, u32[]{:S(2)}) %collective-permute-start.1) | collective-permute-done | bytes 131104 | tf_op jit(solution)/shard_map/ppermute | solution.py:340
  12.2 0.5 collective-permute-start.5
  12.7 1.6 %collective-permute-start.13 = (bf16[2,512,128]{2,1,0:T(8,128)(2,1)S(1)}, bf16[2,512,128]{2,1,0:T(8,128)(2,1)S(1)}, u32[]{:S(2)}, u32[]{:S(2)}) collective-permute-start(bf16[2,512,128]{2,1,0:T(8,128)(2,1)S(1)} %get-tuple-element.41), channel_id=1, source_target_pairs={{0,8},{4,12},{8,24},{12,28},{16,0},{20,4},{24,16},{28,20},{1,9},{5... | collective-permute-start | bytes 786440 | tf_op jit(solution)/shard_map/ppermute | solution.py:337
  14.3 1.9 %collective-permute-start.14 = (bf16[2,512,128]{2,1,0:T(8,128)(2,1)S(1)}, bf16[2,512,128]{2,1,0:T(8,128)(2,1)S(1)}, u32[]{:S(2)}, u32[]{:S(2)}) collective-permute-start(bf16[2,512,128]{2,1,0:T(8,128)(2,1)S(1)} %get-tuple-element.42), channel_id=1, source_target_pairs={{0,12},{4,8},{8,28},{12,24},{16,4},{20,0},{24,20},{28,16},{1,13},{... | collective-permute-start | bytes 786440 | tf_op jit(solution)/shard_map/ppermute | solution.py:337
  16.2 2.2 %copy-done = bf16[2048,1024]{1,0:T(8,128)(2,1)S(1)} copy-done((bf16[2048,1024]{1,0:T(8,128)(2,1)S(1)}, bf16[2048,1024]{1,0:T(8,128)(2,1)}, u32[]{:S(2)}) %copy-start) | copy-done | bytes 4194328
  18.4 1.3 %project.1 = (f32[64,1024]{1,0:T(8,128)S(1)}, f32[64,1024]{1,0:T(8,128)S(1)}, f32[64,1024]{1,0:T(8,128)S(1)}, f32[64,1024]{1,0:T(8,128)S(1)}) custom-call(bf16[64,2048]{1,0:T(8,128)(2,1)S(1)} %get-tuple-element.27.refs_0_, bf16[64,1024]{1,0:T(8,128)(2,1)S(1)} %collective-permute-done.refs_1_, bf16[64,1024]{1,0:T(8,128)(2,1)S(1)} %collective-permute-done.1.refs_2_, ...), custom_call_target="tpu_custom_call" | custom-call | flops 1073741824 | bytes 7340032 | tf_op jit(solution)/shard_map/project/pallas_call | solution.py:113
  19.6 1.3 %collective-permute-start.6 = (f32[64,1024]{1,0:T(8,128)S(1)}, f32[64,1024]{1,0:T(8,128)S(1)}, u32[]{:S(2)}, u32[]{:S(2)}) collective-permute-start(f32[64,1024]{1,0:T(8,128)S(1)} %get-tuple-element.32), channel_id=1, source_target_pairs={{1,0},{0,1},{3,2},{2,3},{5,4},{4,5},{7,6},{6,7},{9,8},{8,9},{11,10... | collective-permute-start | bytes 786440 | tf_op jit(solution)/shard_map/ppermute | solution.py:345
  20.9 0.8 %collective-permute-start.7 = (f32[64,1024]{1,0:T(8,128)S(1)}, f32[64,1024]{1,0:T(8,128)S(1)}, u32[]{:S(2)}, u32[]{:S(2)}) collective-permute-start(f32[64,1024]{1,0:T(8,128)S(1)} %get-tuple-element.33), channel_id=1, source_target_pairs={{2,0},{3,1},{0,2},{1,3},{6,4},{7,5},{4,6},{5,7},{10,8},{11,9},{8,1... | collective-permute-start | bytes 786440 | tf_op jit(solution)/shard_map/ppermute | solution.py:345
  21.8 1.4 %collective-permute-start.8 = (f32[64,1024]{1,0:T(8,128)S(1)}, f32[64,1024]{1,0:T(8,128)S(1)}, u32[]{:S(2)}, u32[]{:S(2)}) collective-permute-start(f32[64,1024]{1,0:T(8,128)S(1)} %get-tuple-element.34), channel_id=1, source_target_pairs={{3,0},{2,1},{1,2},{0,3},{7,4},{6,5},{5,6},{4,7},{11,8},{10,9},{9,1... | collective-permute-start | bytes 786440 | tf_op jit(solution)/shard_map/ppermute | solution.py:345
  23.2 1.6 %shard_map.65 = (bf16[2,512,128]{2,1,0:T(8,128)(2,1)S(1)}, bf16[2,512,128]{2,1,0:T(8,128)(2,1)S(1)}, bf16[2,512,128]{2,1,0:T(8,128)(2,1)S(1)}, bf16[2,512,128]{2...) custom-call(bf16[512,1024]{1,0:T(8,128)(2,1)} %bitcast.5, ...), custom_call_target="tpu_custom_call" | custom-call | bytes 3145728 | tf_op jit(solution)/shard_map/pallas_call | solution.py:79
  24.8 3.5 %collective-permute-start.15 = (bf16[2,512,128]{2,1,0:T(8,128)(2,1)S(1)}, bf16[2,512,128]{2,1,0:T(8,128)(2,1)S(1)}, u32[]{:S(2)}, u32[]{:S(2)}) collective-permute-start(bf16[2,512,128]{2,1,0:T(8,128)(2,1)S(1)} %get-tuple-element.43), channel_id=1, source_target_pairs={{0,24},{4,28},{8,8},{12,12},{16,16},{20,20},{24,0},{28,4},{1,25},{... | collective-permute-start | bytes 786440 | tf_op jit(solution)/shard_map/ppermute | solution.py:337
  28.3 2.5 %collective-permute-start.16 = (bf16[2,512,128]{2,1,0:T(8,128)(2,1)S(1)}, bf16[2,512,128]{2,1,0:T(8,128)(2,1)S(1)}, u32[]{:S(2)}, u32[]{:S(2)}) collective-permute-start(bf16[2,512,128]{2,1,0:T(8,128)(2,1)S(1)} %get-tuple-element.44), channel_id=1, source_target_pairs={{0,28},{4,24},{8,12},{12,8},{16,20},{20,16},{24,4},{28,0},{1,29},{... | collective-permute-start | bytes 786440 | tf_op jit(solution)/shard_map/ppermute | solution.py:337
  30.7 2.9 %collective-permute-done.7.refs_2_ = f32[64,1024]{1,0:T(8,128)S(1)} collective-permute-done((f32[64,1024]{1,0:T(8,128)S(1)}, f32[64,1024]{1,0:T(8,128)S(1)}, u32[]{:S(2)}, u32[]{:S(2)}) %collective-permute-start.7) | collective-permute-done | bytes 262176 | tf_op jit(solution)/shard_map/ppermute | solution.py:345
  33.6 0.4 collective-permute-start.11
  34.1 1.2 %collective-permute-done.8.refs_3_ = f32[64,1024]{1,0:T(8,128)S(1)} collective-permute-done((f32[64,1024]{1,0:T(8,128)S(1)}, f32[64,1024]{1,0:T(8,128)S(1)}, u32[]{:S(2)}, u32[]{:S(2)}) %collective-permute-start.8) | collective-permute-done | bytes 262176 | tf_op jit(solution)/shard_map/ppermute | solution.py:345
  35.3 0.1 round_query.1
  35.3 2.4 %collective-permute-done.15.refs_6_ = bf16[2,512,128]{2,1,0:T(8,128)(2,1)S(1)} collective-permute-done((bf16[2,512,128]{2,1,0:T(8,128)(2,1)S(1)}, bf16[2,512,128]{2,1,0:T(8,128)(2,1)S(1)}, u32[]{:S(2)}, u32[]{:S(2)}) %collective-permute-start.15) | collective-permute-done | bytes 262176 | tf_op jit(solution)/shard_map/ppermute | solution.py:337
  37.8 3.6 %collective-permute-done.16.refs_7_ = bf16[2,512,128]{2,1,0:T(8,128)(2,1)S(1)} collective-permute-done((bf16[2,512,128]{2,1,0:T(8,128)(2,1)S(1)}, bf16[2,512,128]{2,1,0:T(8,128)(2,1)S(1)}, u32[]{:S(2)}, u32[]{:S(2)}) %collective-permute-start.16) | collective-permute-done | bytes 262176 | tf_op jit(solution)/shard_map/ppermute | solution.py:337
  41.4 1.8 %collective-permute-start.17 = (bf16[256,128]{1,0:T(8,128)(2,1)S(1)}, bf16[256,128]{1,0:T(8,128)(2,1)S(1)}, u32[]{:S(2)}, u32[]{:S(2)}) collective-permute-start(bf16[256,128]{1,0:T(8,128)(2,1)S(1)} %get-tuple-element.36.refs_3_.refs_2_), channel_id=1, source_target_pairs={{0,4},{4,0},{8,16},{12,20},{16,8},{20,12},{24,28},{28,24},{1,5},{5... | collective-permute-start | bytes 196616 | tf_op jit(solution)/shard_map/ppermute | solution.py:351
  43.9 1.2 %attend.6 = (f32[144,256]{1,0:T(8,128)S(1)}, bf16[144,256]{1,0:T(8,128)(2,1)S(1)}) custom-call(s32[1]{0:T(128)S(6)} %copy.7.refs_0_, s32[1,64]{1,0:T(1,128)S(1)} %copy-done.1, bf16[256,128]{1,0:T(8,128)(2,1)S(1)} %get-tuple-element.35.refs_2_, bf16[256,128]{1,0:T(8,128)(2,1)S(1)} %collective-permute-done.12.refs_3_, ...), custom_call_target="tpu_custom_call" | custom-call | flops 268435456 | bytes 1048576 | tf_op jit(solution)/shard_map/attend/pallas_call | solution.py:246
  45.1 0.1 collective-permute-start.18
  45.2 1.2 %attend.7 = (f32[144,256]{1,0:T(8,128)S(1)}, bf16[144,256]{1,0:T(8,128)(2,1)S(1)}) custom-call(s32[1]{0:T(128)S(6)} %copy.7.refs_0_, s32[1,64]{1,0:T(1,128)S(1)} %copy-done.1, bf16[256,128]{1,0:T(8,128)(2,1)S(1)} %get-tuple-element.36.refs_3_.refs_2_, bf16[256,128]{1,0:T(8,128)(2,1)S(1)} %collective-permute-done.17.refs_3_, ...), custom_call_target="tpu_custom_call" | custom-call | flops 268435456 | bytes 1048576 | tf_op jit(solution)/shard_map/attend/pallas_call | solution.py:246
  46.4 0.6 collective-permute-start.19
  47.0 1.0 %collective-permute-done.11.refs_6_ = bf16[2,512,128]{2,1,0:T(8,128)(2,1)S(1)} collective-permute-done((bf16[2,512,128]{2,1,0:T(8,128)(2,1)S(1)}, bf16[2,512,128]{2,1,0:T(8,128)(2,1)S(1)}, u32[]{:S(2)}, u32[]{:S(2)}) %collective-permute-start.11) | collective-permute-done | bytes 262176 | tf_op jit(solution)/shard_map/ppermute | solution.py:337
  48.0 1.6 %attend.4.refs_5_ = f32[144,512]{1,0:T(8,128)S(1)} custom-call(s32[1]{0:T(128)S(6)} %copy.7.refs_0_, s32[1,64]{1,0:T(1,128)S(1)} %copy-done.1, bf16[256,128]{1,0:T(8,128)(2,1)S(1)} %get-tuple-element.35.refs_2_, bf16[256,128]{1,0:T(8,128)(2,1)S(1)} %get-tuple-element.36.refs_3_.refs_2_, bf16[2,512,128]{2,1,0:T(8,128)(2,1)S(1)} %get-tuple-element.38.refs_4_, ...), custom_call_target="tpu_custom_call" | custom-call | flops 402653184 | bytes 786432 | tf_op jit(solution)/shard_map/attend/pallas_call | solution.py:246
  49.6 3.8 %collective-permute-done.9.refs_4_ = bf16[2,512,128]{2,1,0:T(8,128)(2,1)S(1)} collective-permute-done((bf16[2,512,128]{2,1,0:T(8,128)(2,1)S(1)}, bf16[2,512,128]{2,1,0:T(8,128)(2,1)S(1)}, u32[]{:S(2)}, u32[]{:S(2)}) %collective-permute-start.9) | collective-permute-done | bytes 262176 | tf_op jit(solution)/shard_map/ppermute | solution.py:337
  53.4 0.8 %attend.5.near_ref = f32[144,512]{1,0:T(8,128)S(1)} custom-call(s32[1]{0:T(128)S(6)} %copy.7.refs_0_, s32[1,64]{1,0:T(1,128)S(1)} %copy-done.1, bf16[256,128]{1,0:T(8,128)(2,1)S(1)} %get-tuple-element.35.refs_2_, bf16[256,128]{1,0:T(8,128)(2,1)S(1)} %get-tuple-element.36.refs_3_.refs_2_, bf16[2,512,128]{2,1,0:T(8,128)(2,1)S(1)} %collective-permute-done.9.refs_4_, ...), custom_call_target="tpu_custom_call" | custom-call | flops 134217728 | bytes 262144 | tf_op jit(solution)/shard_map/attend/pallas_call | solution.py:246
  54.2 0.8 %finish.1 = bf16[64,1024]{1,0:T(8,128)(2,1)} custom-call(f32[144,512]{1,0:T(8,128)S(1)} %attend.5.near_ref, f32[144,256]{1,0:T(8,128)S(1)} %get-tuple-element.45.refs_0_, f32[144,256]{1,0:T(8,128)S(1)} %get-tuple-element.46.refs_1_, bf16[144,256]{1,0:T(8,128)(2,1)S(1)} %collective-permute-done.18.refs_2_, bf16[144,256]{1,0:T(8,128)(2,1)S(1)} %collective-permute-done.19.refs_3_), custom_call_target="tpu_custom_call" | custom-call | flops 524288 | bytes 786432 | tf_op jit(solution)/shard_map/finish/pallas_call | solution.py:295
  (21 shorter events, 0.1 us)
Async XLA Ops:
  1.4 6.9 %collective-permute-start = (bf16[64,1024]{1,0:T(8,128)(2,1)S(1)}, bf16[64,1024]{1,0:T(8,128)(2,1)S(1)}, u32[]{:S(2)}, u32[]{:S(2)}) collective-permute-start(bf16[64,1024]{1,0:T(8,128)(2,1)S(1)} %get-tuple-element.28), channel_id=1, source_target_pairs={{0,1},{1,0},{2,3},{3,2},{4,5},{5,4},{6,7},{7,6},{8,9},{9,8},{10,11... | collective-permute-start | bytes 393224 | tf_op jit(solution)/shard_map/ppermute | solution.py:340
  4.4 7.8 %collective-permute-start.1 = (bf16[64,1024]{1,0:T(8,128)(2,1)S(1)}, bf16[64,1024]{1,0:T(8,128)(2,1)S(1)}, u32[]{:S(2)}, u32[]{:S(2)}) collective-permute-start(bf16[64,1024]{1,0:T(8,128)(2,1)S(1)} %get-tuple-element.29), channel_id=1, source_target_pairs={{0,2},{1,3},{2,0},{3,1},{4,6},{5,7},{6,4},{7,5},{8,10},{9,11},{10,... | collective-permute-start | bytes 393224 | tf_op jit(solution)/shard_map/ppermute | solution.py:340
  5.9 6.3 %collective-permute-start.2 = (bf16[64,1024]{1,0:T(8,128)(2,1)S(1)}, bf16[64,1024]{1,0:T(8,128)(2,1)S(1)}, u32[]{:S(2)}, u32[]{:S(2)}) collective-permute-start(bf16[64,1024]{1,0:T(8,128)(2,1)S(1)} %get-tuple-element.30), channel_id=1, source_target_pairs={{0,3},{1,2},{2,1},{3,0},{4,7},{5,6},{6,5},{7,4},{8,11},{9,10},{10,... | collective-permute-start | bytes 393224 | tf_op jit(solution)/shard_map/ppermute | solution.py:340
  8.3 7.9 %collective-permute-start.3 = (bf16[64,1024]{1,0:T(8,128)(2,1)S(1)}, bf16[64,1024]{1,0:T(8,128)(2,1)S(1)}, u32[]{:S(2)}, u32[]{:S(2)}) collective-permute-start(bf16[64,1024]{1,0:T(8,128)(2,1)S(1)} %collective-permute-done.refs_1_), channel_id=1, source_target_pairs={{0,4},{4,0},{8,12},{12,8},{16,20},{20,16},{24,28},{28,24},{1,5},{5... | collective-permute-start | bytes 393224 | tf_op jit(solution)/shard_map/ppermute | solution.py:341
  12.2 4.0 %collective-permute-start.4 = (bf16[64,1024]{1,0:T(8,128)(2,1)S(1)}, bf16[64,1024]{1,0:T(8,128)(2,1)S(1)}, u32[]{:S(2)}, u32[]{:S(2)}) collective-permute-start(bf16[64,1024]{1,0:T(8,128)(2,1)S(1)} %collective-permute-done.1.refs_2_), channel_id=1, source_target_pairs={{0,4},{4,0},{8,12},{12,8},{16,20},{20,16},{24,28},{28,24},{1,5},{5... | collective-permute-start | bytes 393224 | tf_op jit(solution)/shard_map/ppermute | solution.py:341
  12.2 4.0 %collective-permute-start.5 = (bf16[64,1024]{1,0:T(8,128)(2,1)S(1)}, bf16[64,1024]{1,0:T(8,128)(2,1)S(1)}, u32[]{:S(2)}, u32[]{:S(2)}) collective-permute-start(bf16[64,1024]{1,0:T(8,128)(2,1)S(1)} %collective-permute-done.2.refs_3_), channel_id=1, source_target_pairs={{0,4},{4,0},{8,12},{12,8},{16,20},{20,16},{24,28},{28,24},{1,5},{5... | collective-permute-start | bytes 393224 | tf_op jit(solution)/shard_map/ppermute | solution.py:341
  12.7 12.1 %collective-permute-start.13 = (bf16[2,512,128]{2,1,0:T(8,128)(2,1)S(1)}, bf16[2,512,128]{2,1,0:T(8,128)(2,1)S(1)}, u32[]{:S(2)}, u32[]{:S(2)}) collective-permute-start(bf16[2,512,128]{2,1,0:T(8,128)(2,1)S(1)} %get-tuple-element.41), channel_id=1, source_target_pairs={{0,8},{4,12},{8,24},{12,28},{16,0},{20,4},{24,16},{28,20},{1,9},{5... | collective-permute-start | bytes 786440 | tf_op jit(solution)/shard_map/ppermute | solution.py:337
  14.3 14.0 %collective-permute-start.14 = (bf16[2,512,128]{2,1,0:T(8,128)(2,1)S(1)}, bf16[2,512,128]{2,1,0:T(8,128)(2,1)S(1)}, u32[]{:S(2)}, u32[]{:S(2)}) collective-permute-start(bf16[2,512,128]{2,1,0:T(8,128)(2,1)S(1)} %get-tuple-element.42), channel_id=1, source_target_pairs={{0,12},{4,8},{8,28},{12,24},{16,4},{20,0},{24,20},{28,16},{1,13},{... | collective-permute-start | bytes 786440 | tf_op jit(solution)/shard_map/ppermute | solution.py:337
  16.2 2.2 %copy-start = (bf16[2048,1024]{1,0:T(8,128)(2,1)S(1)}, bf16[2048,1024]{1,0:T(8,128)(2,1)}, u32[]{:S(2)}) copy-start(bf16[2048,1024]{1,0:T(8,128)(2,1)} %refs_7_.1) | copy-start | bytes 12582916
  18.4 25.5 %copy-start.1 = (s32[1,64]{1,0:T(1,128)S(1)}, s32[1,64]{1,0:T(1,128)}, u32[]{:S(2)}) copy-start(s32[1,64]{1,0:T(1,128)} %refs_1_.7) | copy-start | bytes 772
  19.6 11.1 %collective-permute-start.6 = (f32[64,1024]{1,0:T(8,128)S(1)}, f32[64,1024]{1,0:T(8,128)S(1)}, u32[]{:S(2)}, u32[]{:S(2)}) collective-permute-start(f32[64,1024]{1,0:T(8,128)S(1)} %get-tuple-element.32), channel_id=1, source_target_pairs={{1,0},{0,1},{3,2},{2,3},{5,4},{4,5},{7,6},{6,7},{9,8},{8,9},{11,10... | collective-permute-start | bytes 786440 | tf_op jit(solution)/shard_map/ppermute | solution.py:345
  20.9 12.7 %collective-permute-start.7 = (f32[64,1024]{1,0:T(8,128)S(1)}, f32[64,1024]{1,0:T(8,128)S(1)}, u32[]{:S(2)}, u32[]{:S(2)}) collective-permute-start(f32[64,1024]{1,0:T(8,128)S(1)} %get-tuple-element.33), channel_id=1, source_target_pairs={{2,0},{3,1},{0,2},{1,3},{6,4},{7,5},{4,6},{5,7},{10,8},{11,9},{8,1... | collective-permute-start | bytes 786440 | tf_op jit(solution)/shard_map/ppermute | solution.py:345
  21.8 13.5 %collective-permute-start.8 = (f32[64,1024]{1,0:T(8,128)S(1)}, f32[64,1024]{1,0:T(8,128)S(1)}, u32[]{:S(2)}, u32[]{:S(2)}) collective-permute-start(f32[64,1024]{1,0:T(8,128)S(1)} %get-tuple-element.34), channel_id=1, source_target_pairs={{3,0},{2,1},{1,2},{0,3},{7,4},{6,5},{5,6},{4,7},{11,8},{10,9},{9,1... | collective-permute-start | bytes 786440 | tf_op jit(solution)/shard_map/ppermute | solution.py:345
  24.8 13.0 %collective-permute-start.15 = (bf16[2,512,128]{2,1,0:T(8,128)(2,1)S(1)}, bf16[2,512,128]{2,1,0:T(8,128)(2,1)S(1)}, u32[]{:S(2)}, u32[]{:S(2)}) collective-permute-start(bf16[2,512,128]{2,1,0:T(8,128)(2,1)S(1)} %get-tuple-element.43), channel_id=1, source_target_pairs={{0,24},{4,28},{8,8},{12,12},{16,16},{20,20},{24,0},{28,4},{1,25},{... | collective-permute-start | bytes 786440 | tf_op jit(solution)/shard_map/ppermute | solution.py:337
  28.3 13.1 %collective-permute-start.16 = (bf16[2,512,128]{2,1,0:T(8,128)(2,1)S(1)}, bf16[2,512,128]{2,1,0:T(8,128)(2,1)S(1)}, u32[]{:S(2)}, u32[]{:S(2)}) collective-permute-start(bf16[2,512,128]{2,1,0:T(8,128)(2,1)S(1)} %get-tuple-element.44), channel_id=1, source_target_pairs={{0,28},{4,24},{8,12},{12,8},{16,20},{20,16},{24,4},{28,0},{1,29},{... | collective-permute-start | bytes 786440 | tf_op jit(solution)/shard_map/ppermute | solution.py:337
  30.7 16.2 %collective-permute-start.10 = (bf16[2,512,128]{2,1,0:T(8,128)(2,1)S(1)}, bf16[2,512,128]{2,1,0:T(8,128)(2,1)S(1)}, u32[]{:S(2)}, u32[]{:S(2)}) collective-permute-start(bf16[2,512,128]{2,1,0:T(8,128)(2,1)S(1)} %get-tuple-element.39), channel_id=1, source_target_pairs={{0,4},{4,0},{8,12},{12,8},{16,20},{20,16},{24,28},{28,24},{1,5},{5... | collective-permute-start | bytes 786440 | tf_op jit(solution)/shard_map/ppermute | solution.py:337
  33.6 14.3 %collective-permute-start.11 = (bf16[2,512,128]{2,1,0:T(8,128)(2,1)S(1)}, bf16[2,512,128]{2,1,0:T(8,128)(2,1)S(1)}, u32[]{:S(2)}, u32[]{:S(2)}) collective-permute-start(bf16[2,512,128]{2,1,0:T(8,128)(2,1)S(1)} %get-tuple-element.40), channel_id=1, source_target_pairs={{0,8},{4,12},{8,0},{12,4},{16,24},{20,28},{24,16},{28,20},{1,9},{5... | collective-permute-start | bytes 786440 | tf_op jit(solution)/shard_map/ppermute | solution.py:337
  35.3 18.1 %collective-permute-start.9 = (bf16[2,512,128]{2,1,0:T(8,128)(2,1)S(1)}, bf16[2,512,128]{2,1,0:T(8,128)(2,1)S(1)}, u32[]{:S(2)}, u32[]{:S(2)}) collective-permute-start(bf16[2,512,128]{2,1,0:T(8,128)(2,1)S(1)} %get-tuple-element.37), channel_id=1, source_target_pairs={{0,12},{4,8},{8,4},{12,0},{16,28},{20,24},{24,20},{28,16},{1,13},{... | collective-permute-start | bytes 786440 | tf_op jit(solution)/shard_map/ppermute | solution.py:337
  37.8 6.1 %collective-permute-start.12 = (bf16[256,128]{1,0:T(8,128)(2,1)S(1)}, bf16[256,128]{1,0:T(8,128)(2,1)S(1)}, u32[]{:S(2)}, u32[]{:S(2)}) collective-permute-start(bf16[256,128]{1,0:T(8,128)(2,1)S(1)} %get-tuple-element.35.refs_2_), channel_id=1, source_target_pairs={{0,4},{4,0},{8,16},{12,20},{16,8},{20,12},{24,28},{28,24},{1,5},{5... | collective-permute-start | bytes 196616 | tf_op jit(solution)/shard_map/ppermute | solution.py:351
  41.4 3.8 %collective-permute-start.17 = (bf16[256,128]{1,0:T(8,128)(2,1)S(1)}, bf16[256,128]{1,0:T(8,128)(2,1)S(1)}, u32[]{:S(2)}, u32[]{:S(2)}) collective-permute-start(bf16[256,128]{1,0:T(8,128)(2,1)S(1)} %get-tuple-element.36.refs_3_.refs_2_), channel_id=1, source_target_pairs={{0,4},{4,0},{8,16},{12,20},{16,8},{20,12},{24,28},{28,24},{1,5},{5... | collective-permute-start | bytes 196616 | tf_op jit(solution)/shard_map/ppermute | solution.py:351
  45.1 9.1 %collective-permute-start.18 = (bf16[144,256]{1,0:T(8,128)(2,1)S(1)}, bf16[144,256]{1,0:T(8,128)(2,1)S(1)}, u32[]{:S(2)}, u32[]{:S(2)}) collective-permute-start(bf16[144,256]{1,0:T(8,128)(2,1)S(1)} %get-tuple-element.47), channel_id=1, source_target_pairs={{0,4},{4,0},{8,16},{12,20},{16,8},{20,12},{24,28},{28,24},{1,5},{5... | collective-permute-start | bytes 221192 | tf_op jit(solution)/shard_map/ppermute | solution.py:355
  46.4 7.8 %collective-permute-start.19 = (bf16[144,256]{1,0:T(8,128)(2,1)S(1)}, bf16[144,256]{1,0:T(8,128)(2,1)S(1)}, u32[]{:S(2)}, u32[]{:S(2)}) collective-permute-start(bf16[144,256]{1,0:T(8,128)(2,1)S(1)} %get-tuple-element.48), channel_id=1, source_target_pairs={{0,4},{4,0},{8,16},{12,20},{16,8},{20,12},{24,28},{28,24},{1,5},{5... | collective-permute-start | bytes 221192 | tf_op jit(solution)/shard_map/ppermute | solution.py:355
